TPU v7x, 256 devices: a whole 4x4x8 slice. The times are simulated.
256 devices in a mesh: row: 16 (over y, x), col: 16 (over z, core).
Axes of the slice: x: 4, y: 4, z: 8, core: 2. Of those that a mesh axis runs over, the one named last changes fastest.
Arguments:
- block_values: float32 [16, 16, 40, 128, 128], P('row', 'col'), may hold values from 7.8125e-06 to 0.00078125
- block_index: int32 [16, 16, 2, 40], P('row', 'col'), may hold values from 0 to 31, as said below
- block_count: int32 [16, 16], P('row', 'col'), may hold values from 1 to 40, as said below
- strength: float32 [32], replicated, may hold values from 1 to 30
- raw_scores: float32 [512, 32, 128], P(('row', 'col')), may hold values from -24 to 24
Outputs:
- smoothed: float32 [512, 32, 128], P(('row', 'col'))
- final_residual: float32 [512, 32, 128], P(('row', 'col'))
Inputs may be any that keep to these rules, and one draw needn't show every extreme that they name: `block_count`: some device has exactly 40 live slots; the others hold between half and all of their share of the upper triangle, scaled to 40. `block_index`: the live slots of one device name distinct blocks, each with global block row at most its global block column; slots at or above the count hold pairs in range that are ignored.
All inputs are finite; a program needn't handle non-finite values.
Results may differ from a plain program's by a relative error of at most 0.0003.
Values sent between devices are 32-bit elements; how exact they have to be, the bound alone decides.
A program may use at most 64 MiB of HBM per device.

v0:
```python
import jax
import jax.numpy as jnp
from jax import lax
from jax.sharding import PartitionSpec as P

ITERS = 3


def local_terms(values, row_index, col_index, panel_rows, panel_cols):
    picked_cols = jnp.take(panel_cols, col_index, axis=0)
    picked_rows = jnp.take(panel_rows, row_index, axis=0)
    to_rows = jnp.einsum("crk,cik->cri", picked_cols, values, precision=lax.Precision.HIGHEST)
    to_cols = jnp.einsum("cri,cik->crk", picked_rows, values, precision=lax.Precision.HIGHEST)
    row_part = jax.ops.segment_sum(to_rows, row_index, num_segments=panel_rows.shape[0])
    col_part = jax.ops.segment_sum(to_cols, col_index, num_segments=panel_cols.shape[0])
    return (row_part, col_part)


def fold_terms(row_part, col_part):
    return lax.psum_scatter(row_part, "col", scatter_dimension=0, tiled=True) + lax.psum_scatter(
        col_part, "row", scatter_dimension=0, tiled=True
    )


def total(field):
    return jnp.sum(field, axis=(0, 2))


def global_sum(partial_sum):
    return lax.psum(partial_sum, ("row", "col"))


def shards(block_values, block_index, block_count, strength, raw_scores):
    values = block_values[0, 0]
    row_index = block_index[0, 0, 0]
    col_index = block_index[0, 0, 1]
    live_mask = (jnp.arange(values.shape[0], dtype=jnp.int32) < block_count[0, 0]).astype(
        jnp.float32
    )
    masked = values * live_mask[:, None, None]
    segment = raw_scores.shape[0]
    block_size = raw_scores.shape[2]
    rows_here = lax.axis_size("col") * segment
    cols_here = lax.axis_size("row") * segment
    ones_rows = jnp.ones((rows_here, 1, block_size), jnp.float32)
    ones_cols = jnp.ones((cols_here, 1, block_size), jnp.float32)
    degree_rows, degree_cols = local_terms(masked, row_index, col_index, ones_rows, ones_cols)
    degree = fold_terms(degree_rows, degree_cols)
    gains = strength[None, :, None]
    smoothed = jnp.zeros_like(raw_scores)
    residual = raw_scores
    direction = raw_scores
    norm_now = global_sum(total(residual * residual))
    for iteration in range(ITERS):
        panel_rows = lax.all_gather(direction, "col", axis=0, tiled=True)
        panel_cols = lax.all_gather(direction, "row", axis=0, tiled=True)
        row_part, col_part = local_terms(masked, row_index, col_index, panel_rows, panel_cols)
        product = fold_terms(row_part, col_part)
        image = direction + gains * (degree * direction - product)
        step_size = norm_now / global_sum(total(direction * image))
        smoothed = smoothed + step_size[None, :, None] * direction
        residual = residual - step_size[None, :, None] * image
        norm_next = global_sum(total(residual * residual))
        direction = residual + (norm_next / norm_now)[None, :, None] * direction
        norm_now = norm_next
    return (smoothed, residual)


def solution(mesh):
    placed = (
        P("row", "col", None, None, None),
        P("row", "col", None, None),
        P("row", "col"),
        P(),
        P(("row", "col"), None, None),
    )
    return jax.shard_map(
        shards,
        mesh=mesh,
        in_specs=placed,
        out_specs=(P(("row", "col"), None, None), P(("row", "col"), None, None)),
        check_vma=False,
    )
```

profile of v0, /device:TPU:1, one launch (start us, length us, event | category | flops | bytes accessed | tf_op | source)
XLA Modules:
  0.0 916.9 jit_solution(5695150841030016190)
XLA Ops:
  7.2 0.8 compare_and_fusion
  8.0 0.8 slice_bitcast_fusion
  9.4 23.0 %all_gather.19 = f32[32,32,128]{2,1,0:T(8,128)S(1)} all-gather(f32[2,32,128]{2,1,0:T(8,128)} %param.13), channel_id=1, replica_groups=mesh['row'=16,'col'=16] {'col'}, dimensions={0}, use_global_device_ids=true | all-gather | bytes 557056 | tf_op jit(solution)/shard_map/all_gather | solution.py:55
  32.4 0.6 gather_fusion.3
  33.0 5.0 fusion.4
  38.1 4.9 scatter_fusion.1
  43.0 0.8 copy-done.3
  43.8 0.0 reduce-scatter.9.cloned.1.call-start
  43.9 19.6 %all_gather.18 = f32[32,32,128]{2,1,0:T(8,128)S(1)} all-gather(f32[2,32,128]{2,1,0:T(8,128)S(1)} %copy-done.7), channel_id=1, replica_groups=mesh['row'=16,'col'=16] {'row'}, dimensions={0}, use_global_device_ids=true | all-gather | bytes 557056 | tf_op jit(solution)/shard_map/all_gather | solution.py:56
  63.5 1.4 gather_fusion.2
  64.9 6.2 fusion.5
  71.1 4.7 scatter_fusion
  75.9 0.8 copy-done.4
  76.7 0.0 reduce-scatter.15.cloned.1.call-start
  76.7 0.6 gather_fusion
  77.3 0.6 gather_fusion.1
  77.9 0.6 dynamic-slice
  78.5 0.6 dynamic-slice.2
  80.4 0.1 bitcast_select_fusion
  80.5 4.3 fusion.7
  84.7 0.9 scatter_custom_fusion
  85.7 2.3 fusion.6
  88.0 0.7 scatter_custom_fusion.1
  88.7 58.4 %all-reduce.1 = f32[32,1,128]{2,0,1:T(8,128)S(1)} all-reduce(f32[32,1,128]{2,0,1:T(8,128)S(1)} %bitcast.49), channel_id=3, replica_groups=mesh['row'=16,'col'=16] {'row'}, use_global_device_ids=true, to_apply=%region_5.7.clone | all-reduce | flops 4096 | bytes 32768
  147.1 61.3 %all-reduce = f32[32,1,128]{2,0,1:T(8,128)S(1)} all-reduce(f32[32,1,128]{2,0,1:T(8,128)S(1)} %bitcast.48), channel_id=2, replica_groups=mesh['row'=16,'col'=16] {'col'}, use_global_device_ids=true, to_apply=%region_3.5.clone | all-reduce | flops 4096 | bytes 32768
  208.5 1.0 multiply_reduce_fusion.4
  209.4 74.0 %all-reduce.2 = (f32[32]{0:T(128)S(1)}, f32[32]{0:T(128)S(1)}) all-reduce(f32[32]{0:T(128)S(1)} %get-tuple-element.5, f32[32]{0:T(128)S(1)} %get-tuple-element.4), channel_id=1, replica_groups=mesh['row'=16,'col'=16] {'row','col'}, use_global_device_ids=true, to_apply=%region_1.2 | all-reduce | flops 64 | bytes 512 | tf_op jit(solution)/shard_map/psum | solution.py:30
  283.5 1.0 multiply_reduce_fusion.3
  284.4 74.5 %psum.44 = f32[32]{0:T(128)S(1)} all-reduce(f32[32]{0:T(128)S(1)} %get-tuple-element.10), channel_id=1, replica_groups=mesh['row'=16,'col'=16] {'row','col'}, use_global_device_ids=true, to_apply=%region_13.16 | all-reduce | flops 32 | bytes 256 | tf_op jit(solution)/shard_map/psum | solution.py:30
  358.9 0.1 multiply_add_fusion.4
  359.0 17.2 %all_gather.21 = f32[32,32,128]{2,1,0:T(8,128)S(1)} all-gather(f32[2,32,128]{2,1,0:T(8,128)S(1)} %multiply_add_fusion.4), channel_id=1, replica_groups=mesh['row'=16,'col'=16] {'col'}, dimensions={0}, use_global_device_ids=true | all-gather | bytes 557056 | tf_op jit(solution)/shard_map/all_gather | solution.py:55
  376.2 1.4 gather_fusion.5
  377.6 4.3 fusion.2
  382.0 4.7 scatter_fusion.3
  386.7 0.8 copy-done.5
  387.6 0.0 reduce-scatter.13.cloned.1.call-start
  387.6 19.2 %all_gather.20 = f32[32,32,128]{2,1,0:T(8,128)S(1)} all-gather(f32[2,32,128]{2,1,0:T(8,128)S(1)} %multiply_add_fusion.4), channel_id=1, replica_groups=mesh['row'=16,'col'=16] {'row'}, dimensions={0}, use_global_device_ids=true | all-gather | bytes 557056 | tf_op jit(solution)/shard_map/all_gather | solution.py:56
  406.8 1.4 gather_fusion.4
  408.3 6.2 fusion.3
  414.5 4.7 scatter_fusion.2
  419.2 0.8 copy-done.6
  420.1 38.4 %reduce-scatter.15.cloned.1.call-done = f32[2,32,128]{2,1,0:T(8,128)} async-done(((f32[32,32,128]{2,1,0:T(8,128)}), f32[2,32,128]{2,1,0:T(8,128)}) %reduce-scatter.15.cloned.1.call-update) | async-done | bytes 32784 | tf_op jit(solution)/shard_map/reduce_scatter | solution.py:20
  458.4 57.2 %reduce-scatter.13.cloned.1.call-done = f32[2,32,128]{2,1,0:T(8,128)} async-done(((f32[32,32,128]{2,1,0:T(8,128)}), f32[2,32,128]{2,1,0:T(8,128)}) %reduce-scatter.13.cloned.1.call-update) | async-done | bytes 32784 | tf_op jit(solution)/shard_map/reduce_scatter | solution.py:20
  515.7 1.0 multiply_reduce_fusion.2
  516.6 79.6 %psum.45 = f32[32]{0:T(128)S(1)} all-reduce(f32[32]{0:T(128)S(1)} %multiply_reduce_fusion.2), channel_id=1, replica_groups=mesh['row'=16,'col'=16] {'row','col'}, use_global_device_ids=true, to_apply=%region_19.22 | all-reduce | flops 32 | bytes 256 | tf_op jit(solution)/shard_map/psum | solution.py:30
  596.2 1.0 multiply_reduce_fusion.1
  597.2 72.4 %psum.46 = f32[32]{0:T(128)S(1)} all-reduce(f32[32]{0:T(128)S(1)} %get-tuple-element.8), channel_id=1, replica_groups=mesh['row'=16,'col'=16] {'row','col'}, use_global_device_ids=true, to_apply=%region_21.24 | all-reduce | flops 32 | bytes 256 | tf_op jit(solution)/shard_map/psum | solution.py:30
  669.5 0.1 multiply_add_fusion.2
  669.6 18.1 %all_gather.23 = f32[32,32,128]{2,1,0:T(8,128)S(1)} all-gather(f32[2,32,128]{2,1,0:T(8,128)S(1)} %multiply_add_fusion.2), channel_id=1, replica_groups=mesh['row'=16,'col'=16] {'col'}, dimensions={0}, use_global_device_ids=true | all-gather | bytes 557056 | tf_op jit(solution)/shard_map/all_gather | solution.py:55
  687.7 1.4 gather_fusion.7
  689.1 4.3 fusion
  693.5 4.7 scatter_fusion.5
  698.3 0.8 copy-done.2
  699.1 19.2 %all_gather.22 = f32[32,32,128]{2,1,0:T(8,128)S(1)} all-gather(f32[2,32,128]{2,1,0:T(8,128)S(1)} %multiply_add_fusion.2), channel_id=1, replica_groups=mesh['row'=16,'col'=16] {'row'}, dimensions={0}, use_global_device_ids=true | all-gather | bytes 557056 | tf_op jit(solution)/shard_map/all_gather | solution.py:56
  718.3 1.4 gather_fusion.6
  719.8 5.3 fusion.1
  725.1 0.1 broadcast.50.clone.4
  725.2 2.7 scatter_fusion.4
  727.8 0.8 copy-done.1
  728.6 41.9 %reduce-scatter.19.cloned.1.call-done = f32[2,32,128]{2,1,0:T(8,128)} async-done(((f32[32,32,128]{2,1,0:T(8,128)}), f32[2,32,128]{2,1,0:T(8,128)}) %reduce-scatter.19.cloned.1.call-update) | async-done | bytes 32784 | tf_op jit(solution)/shard_map/reduce_scatter | solution.py:20
  770.6 57.2 %reduce-scatter.17.cloned.1.call-done = f32[2,32,128]{2,1,0:T(8,128)} async-done(((f32[32,32,128]{2,1,0:T(8,128)}), f32[2,32,128]{2,1,0:T(8,128)}) %reduce-scatter.17.cloned.1.call-update) | async-done | bytes 32784 | tf_op jit(solution)/shard_map/reduce_scatter | solution.py:20
  827.8 1.0 multiply_reduce_fusion
  828.7 79.8 %psum.47 = f32[32]{0:T(128)S(1)} all-reduce(f32[32]{0:T(128)S(1)} %multiply_reduce_fusion), channel_id=1, replica_groups=mesh['row'=16,'col'=16] {'row','col'}, use_global_device_ids=true, to_apply=%region_27.30 | all-reduce | flops 32 | bytes 256 | tf_op jit(solution)/shard_map/psum | solution.py:30
  908.5 1.5 multiply_subtract_fusion
  (42 shorter events, 0.6 us)
Async XLA Ops:
  7.2 201.3 %reduce-scatter.11.cloned.1.call-start = ((), (), s32[]{:S(2)}) async-start(), calls=%async_computation.7 | async-start | bytes 557056 | tf_op jit(solution)/shard_map/reduce_scatter | solution.py:20
  33.0 10.9 %copy-start.7 = (f32[2,32,128]{2,1,0:T(8,128)S(1)}, f32[2,32,128]{2,1,0:T(8,128)}, u32[]{:S(2)}) copy-start(f32[2,32,128]{2,1,0:T(8,128)} %param.13) | copy-start | bytes 98308
  38.0 26.9 %copy-start = (f32[1,1,40,128,128]{4,3,2,1,0:T(8,128)S(1)}, f32[1,1,40,128,128]{4,3,2,1,0:T(8,128)}, u32[]{:S(2)}) copy-start(f32[1,1,40,128,128]{4,3,2,1,0:T(8,128)} %param.9) | copy-start | bytes 7864324
  42.9 0.8 copy-start.3
  43.8 164.7 %reduce-scatter.9.cloned.1.call-start = ((), (), s32[]{:S(2)}) async-start(), calls=%async_computation.6 | async-start | bytes 557056 | tf_op jit(solution)/shard_map/reduce_scatter | solution.py:20
  71.1 6.8 copy-start.10
  71.1 7.4 copy-start.9
  75.9 0.8 copy-start.4
  76.7 381.8 %reduce-scatter.15.cloned.1.call-start = ((), (), s32[]{:S(2)}) async-start(), calls=%async_computation.9 | async-start | bytes 557056 | tf_op jit(solution)/shard_map/reduce_scatter | solution.py:20
  80.5 128.0 %copy-start.8 = (f32[32]{0:T(128)S(1)}, f32[32]{0:T(128)}, u32[]{:S(2)}) copy-start(f32[32]{0:T(128)} %param.12) | copy-start | bytes 388
  386.7 0.8 copy-start.5
  387.6 128.1 %reduce-scatter.13.cloned.1.call-start = ((), (), s32[]{:S(2)}) async-start(), calls=%async_computation.8 | async-start | bytes 557056 | tf_op jit(solution)/shard_map/reduce_scatter | solution.py:20
  419.2 0.8 copy-start.6
  420.0 350.6 %reduce-scatter.19.cloned.1.call-start = ((), (), s32[]{:S(2)}) async-start(), calls=%async_computation.11 | async-start | bytes 557056 | tf_op jit(solution)/shard_map/reduce_scatter | solution.py:20
  698.3 0.8 copy-start.2
  699.1 128.7 %reduce-scatter.17.cloned.1.call-start = ((), (), s32[]{:S(2)}) async-start(), calls=%async_computation.10 | async-start | bytes 557056 | tf_op jit(solution)/shard_map/reduce_scatter | solution.py:20
  727.8 0.8 copy-start.1
Sparse Core Ops, SparseCore 0:
  43.9 73.3 reduce-scatter.10
  120.0 55.2 reduce-scatter.8
  387.7 70.6 reduce-scatter.14
  460.9 54.6 reduce-scatter.12
  699.2 71.3 reduce-scatter.18
  773.1 54.6 reduce-scatter.16
where the time goes:
time: 918 us; the launch traced here: 917 us
  blocking collectives  616 us (67%)
  waiting for transfers between devices  195 us (21%)
  matrix products  37.9 us (4%)
  other arithmetic  35.3 us (4%)
  between operations  16.3 us (2%)
  local copies, waits for them, and re-layouts  15.9 us (2%)
    psum x5, blocking collectives, global_sum(): return lax.psum(partial_sum, ('row', 'col'))  380 us
    unnamed x2, blocking collectives  120 us
    reduce_scatter x3, waiting for transfers between devices, fold_terms(): lax.psum_scatter(row_part, 'col', scatter_dimension=0, tiled=True)  114 us
    reduce_scatter x3, waiting for transfers between devices, fold_terms(): lax.psum_scatter(col_part, 'row', scatter_dimension=0, tiled=True)  80.3 us
    all_gather x3, blocking collectives, shards(): panel_rows = lax.all_gather(direction, 'col', axis=0, tiled=True)  58.3 us
    all_gather x3, blocking collectives, shards(): panel_cols = lax.all_gather(direction, 'row', axis=0, tiled=True)  58 us
    dot_general x4, matrix products, local_terms(): jnp.einsum('crk,cik->cri', picked_cols, values, precision=lax.Precision.H...  22 us
  transfers between devices with their start and end apart: 6, of which 4 were waited for; matrix products, arithmetic and copies ran while one was open for 5% of the time, Pallas kernels for 0%

commit v1 on v0

v1 whole, which is shorter than its diff:
```python
import functools

import jax
import jax.numpy as jnp
from jax import lax
from jax.experimental import pallas as pl
from jax.experimental.pallas import tpu as pltpu
from jax.sharding import PartitionSpec as P

ITERS = 3
MESH = pl.DeviceIdType.MESH
F32 = jnp.float32
BF16 = jnp.bfloat16


def split(x):
    high = x.astype(BF16)
    low = (x - high.astype(F32)).astype(BF16)
    return high, low


def product(field, weights):
    size = field.shape[0]
    width = field.shape[1]
    high, low = split(field)
    both = jnp.concatenate([high, low], axis=0)
    out = jnp.dot(both, weights, preferred_element_type=F32)
    upper = out[:size, :width]
    return upper + ((out[size:, :width] + out[:size, width:]) + out[size:, width:])


def body(
    n_row,
    n_col,
    values_hbm,
    order,
    keep,
    index_ref,
    live_ref,
    gain_ref,
    raw_ref,
    smooth_ref,
    resid_ref,
    *scratch,
):
    names = iter(scratch)
    take = lambda: next(names)
    stored, natural, turned, sums_row, sums_col = take(), take(), take(), take(), take()
    running, row_part, col_part = take(), take(), take()
    resid, degree, direct, image = take(), take(), take(), take()
    panel_rows = [take() for _ in range(ITERS)]
    panel_cols = [take() for _ in range(ITERS)]
    row_send = [take() for _ in range(ITERS)]
    col_send = [take() for _ in range(ITERS)]
    row_got = [take() for _ in range(ITERS)]
    col_got = [take() for _ in range(ITERS)]
    dot_own = [take() for _ in range(ITERS)]
    dot_line = [take() for _ in range(ITERS)]
    dot_col_got = [take() for _ in range(ITERS)]
    dot_row_got = [take() for _ in range(ITERS)]
    deg_row_send, deg_col_send, deg_row_got, deg_col_got = take(), take(), take(), take()
    value_sem = take()
    sent = take()
    got = take()

    a = lax.axis_index("row")
    c = lax.axis_index("col")
    cap = stored.shape[0]
    size = stored.shape[1]
    seg = raw_ref.shape[0]
    rhs = raw_ref.shape[1]
    n_local = n_col * seg
    n_other = n_row * seg

    fetch = pltpu.make_async_copy(values_hbm.at[0, 0], stored, value_sem)
    fetch.start()

    barrier = pltpu.get_barrier_semaphore()

    def greet_col(k, _):
        pl.semaphore_signal(
            barrier, inc=1, device_id=(a, lax.rem(c + k, n_col)), device_id_type=MESH
        )
        return 0

    def greet_row(k, _):
        pl.semaphore_signal(
            barrier, inc=1, device_id=(lax.rem(a + k, n_row), c), device_id_type=MESH
        )
        return 0

    lax.fori_loop(1, n_col, greet_col, 0)
    lax.fori_loop(1, n_row, greet_row, 0)
    resid[0] = raw_ref[...]
    panel_rows[0][pl.ds(seg * c, seg)] = raw_ref[...]
    panel_cols[0][pl.ds(seg * a, seg)] = raw_ref[...]
    pl.semaphore_wait(barrier, n_col + n_row - 2)

    def along_col(src, dst, peer, which):
        return pltpu.make_async_remote_copy(
            src_ref=src,
            dst_ref=dst,
            send_sem=sent.at[which, peer],
            recv_sem=got.at[which, c],
            device_id=(a, peer),
            device_id_type=MESH,
        )

    def along_row(src, dst, peer, which):
        return pltpu.make_async_remote_copy(
            src_ref=src,
            dst_ref=dst,
            send_sem=sent.at[which, peer],
            recv_sem=got.at[which, a],
            device_id=(peer, c),
            device_id_type=MESH,
        )

    def each_col(act):
        lax.fori_loop(1, n_col, lambda k, _: (act(lax.rem(c + k, n_col)), 0)[1], 0)

    def each_row(act):
        lax.fori_loop(1, n_row, lambda k, _: (act(lax.rem(a + k, n_row)), 0)[1], 0)

    def rows_below(act):
        lax.fori_loop(0, a, lambda k, _: (act(k), 0)[1], 0)

    def rows_above(act):
        lax.fori_loop(a + 1, n_row, lambda k, _: (act(k), 0)[1], 0)

    def arrive(dst, peer, which):
        pltpu.make_async_copy(dst, dst, got.at[which, peer]).wait()

    def leave(src, peer, which):
        pltpu.make_async_copy(src, src, sent.at[which, peer]).wait()

    GATHER_COL, GATHER_ROW, PART_COL, PART_ROW, DOT_COL, DOT_ROW = range(6)
    DEG_COL, DEG_ROW = 6 * ITERS, 6 * ITERS + 1

    def gather(step):
        def to_row(peer):
            along_row(
                resid.at[step],
                panel_cols[step].at[pl.ds(seg * a, seg)],
                peer,
                6 * step + GATHER_ROW,
            ).start()

        def to_col(peer):
            along_col(
                resid.at[step],
                panel_rows[step].at[pl.ds(seg * c, seg)],
                peer,
                6 * step + GATHER_COL,
            ).start()

        rows_below(to_row)
        each_col(to_col)

    gather(0)
    fetch.wait()

    def prepare(q, _):
        block = stored[q]
        flipped = block.T
        high, low = split(block)
        natural[q, :, :size] = high
        natural[q, :, size:] = low
        high, low = split(flipped)
        turned[q, :, :size] = high
        turned[q, :, size:] = low
        sums_row[pl.ds(q, 1), :] = jnp.sum(flipped, axis=0, keepdims=True)
        sums_col[pl.ds(q, 1), :] = jnp.sum(block, axis=0, keepdims=True)
        return 0

    lax.fori_loop(0, cap, prepare, 0, unroll=2)

    live = live_ref[...]

    def pick(line, count):
        wanted = lax.broadcasted_iota(jnp.int32, (count, cap), 0)
        return jnp.where(wanted == index_ref[line : line + 1, :], live, 0.0)

    degree_rows = jnp.dot(
        pick(0, n_local), sums_row[...], precision=lax.Precision.HIGHEST, preferred_element_type=F32
    )
    degree_cols = jnp.dot(
        pick(1, n_other), sums_col[...], precision=lax.Precision.HIGHEST, preferred_element_type=F32
    )
    for peer in range(n_col):
        deg_row_send[peer, 0:seg, :] = degree_rows[seg * peer : seg * peer + seg, :]
    for peer in range(n_row):
        deg_col_send[peer, 0:seg, :] = degree_cols[seg * peer : seg * peer + seg, :]
    each_col(lambda peer: along_col(deg_row_send.at[peer], deg_row_got.at[c], peer, DEG_COL).start())
    rows_above(lambda peer: along_row(deg_col_send.at[peer], deg_col_got.at[a], peer, DEG_ROW).start())
    deg_row_got[c] = deg_row_send[c]
    deg_col_got[a] = deg_col_send[a]

    gains = gain_ref[...]

    def pass_over(weights, panel, base, limit):
        def slot(k, total):
            weight = weights[order[base + k]]
            field = panel[order[base + cap + k]]
            total = total * keep[limit + k] + product(field, weight)
            running[k] = total
            return total

        lax.fori_loop(0, cap, slot, jnp.zeros((rhs, size), F32), unroll=4)

    def total_of(ref, count):
        out = ref[0]
        for k in range(1, count):
            out = out + ref[k]
        return out

    gamma_old = None
    alpha_old = None
    smooth = None
    for step in range(ITERS):
        rows_above(lambda peer: arrive(panel_cols[step].at[pl.ds(seg * peer, seg)], peer, 6 * step + GATHER_ROW))
        pass_over(turned, panel_cols[step], 0, 0)
        for u in range(n_local):
            row_send[step][u] = running[order[4 * cap + u]] * keep[2 * cap + u]
        each_col(
            lambda peer: along_col(
                row_send[step].at[pl.ds(seg * peer, seg)],
                row_got[step].at[pl.ds(seg * c, seg)],
                peer,
                6 * step + PART_COL,
            ).start()
        )
        row_got[step][pl.ds(seg * c, seg)] = row_send[step][pl.ds(seg * c, seg)]
        each_col(lambda peer: arrive(panel_rows[step].at[pl.ds(seg * peer, seg)], peer, 6 * step + GATHER_COL))
        if step == 0:
            each_col(lambda peer: arrive(deg_row_got.at[peer], peer, DEG_COL))
            rows_below(lambda peer: arrive(deg_col_got.at[peer], peer, DEG_ROW))
            here = total_of(deg_row_got, n_col)
            here = here + lax.fori_loop(
                0, a + 1, lambda k, t: t + deg_col_got[k], jnp.zeros_like(here)
            )
            for j in range(seg):
                degree[j] = jnp.broadcast_to(here[j : j + 1, :], (rhs, size))
        own = resid[step]
        square = own * own
        cross = panel_rows[step][0] * row_send[step][0]
        for u in range(1, n_local):
            cross = cross + panel_rows[step][u] * row_send[step][u]
        gamma_part = square[0]
        delta_part = degree[0] * square[0]
        for j in range(1, seg):
            gamma_part = gamma_part + square[j]
            delta_part = delta_part + degree[j] * square[j]
        delta_part = gamma_part + gains * (delta_part - 2.0 * cross)
        parts = jnp.concatenate([gamma_part, delta_part, jnp.zeros((size - 2 * rhs, size), F32)], axis=0)
        summed = jnp.sum(parts.T, axis=0, keepdims=True)
        dot_own[step][...] = jnp.broadcast_to(summed, (8, size))
        each_col(lambda peer: along_col(dot_own[step], dot_col_got[step].at[c], peer, 6 * step + DOT_COL).start())
        dot_col_got[step][c] = dot_own[step][...]

        pass_over(natural, panel_rows[step], 2 * cap, cap)
        for v in range(n_other):
            col_send[step][v] = running[order[4 * cap + n_local + v]] * keep[2 * cap + n_local + v]
        rows_above(
            lambda peer: along_row(
                col_send[step].at[pl.ds(seg * peer, seg)],
                col_got[step].at[pl.ds(seg * a, seg)],
                peer,
                6 * step + PART_ROW,
            ).start()
        )
        col_got[step][pl.ds(seg * a, seg)] = col_send[step][pl.ds(seg * a, seg)]

        each_col(lambda peer: arrive(dot_col_got[step].at[peer], peer, 6 * step + DOT_COL))
        dot_line[step][...] = total_of(dot_col_got[step], n_col)
        each_row(lambda peer: along_row(dot_line[step], dot_row_got[step].at[a], peer, 6 * step + DOT_ROW).start())
        dot_row_got[step][a] = dot_line[step][...]

        each_col(lambda peer: arrive(row_got[step].at[pl.ds(seg * peer, seg)], peer, 6 * step + PART_COL))
        spread = []
        for j in range(seg):
            out = row_got[step][j]
            for k in range(1, n_col):
                out = out + row_got[step][seg * k + j]
            spread.append(out)
        rows_below(lambda peer: arrive(col_got[step].at[pl.ds(seg * peer, seg)], peer, 6 * step + PART_ROW))

        def add_cols(k, both):
            return tuple(both[j] + col_got[step][seg * k + j] for j in range(seg))

        spread = lax.fori_loop(0, a + 1, add_cols, tuple(spread))

        each_row(lambda peer: arrive(dot_row_got[step].at[peer], peer, 6 * step + DOT_ROW))
        dots = total_of(dot_row_got[step], n_row)
        dots = jnp.concatenate([dots] * (size // 8), axis=0).T
        gamma = dots[:rhs, 0:1]
        delta = dots[rhs : 2 * rhs, 0:1]
        if step == 0:
            alpha = gamma / delta
            beta = None
        else:
            beta = gamma / gamma_old
            alpha = gamma / (delta - beta * gamma / alpha_old)
        for j in range(seg):
            r = own[j]
            w = r + gains * (degree[j] * r - spread[j])
            if step == 0:
                d, ad = r, w
                x = alpha * d
            else:
                d = r + beta * direct[j]
                ad = w + beta * image[j]
                x = smooth_ref[j] + alpha * d
            nxt = r - alpha * ad
            smooth_ref[j] = x
            if step < ITERS - 1:
                direct[j] = d
                image[j] = ad
                resid[step + 1, j] = nxt
            else:
                resid_ref[j] = nxt
        if step < ITERS - 1:
            panel_rows[step + 1][pl.ds(seg * c, seg)] = resid[step + 1]
            panel_cols[step + 1][pl.ds(seg * a, seg)] = resid[step + 1]
            gather(step + 1)
        gamma_old, alpha_old = gamma, alpha

    for step in range(ITERS):
        rows_below(lambda peer: leave(resid.at[step], peer, 6 * step + GATHER_ROW))
        each_col(lambda peer: leave(resid.at[step], peer, 6 * step + GATHER_COL))
        each_col(lambda peer: leave(row_send[step].at[pl.ds(seg * peer, seg)], peer, 6 * step + PART_COL))
        rows_above(lambda peer: leave(col_send[step].at[pl.ds(seg * peer, seg)], peer, 6 * step + PART_ROW))
        each_col(lambda peer: leave(dot_own[step], peer, 6 * step + DOT_COL))
        each_row(lambda peer: leave(dot_line[step], peer, 6 * step + DOT_ROW))
    each_col(lambda peer: leave(deg_row_send.at[peer], peer, DEG_COL))
    rows_above(lambda peer: leave(deg_col_send.at[peer], peer, DEG_ROW))


def plan(line, other, count, groups):
    cap = line.shape[0]
    slot = jnp.arange(cap, dtype=jnp.int32)
    live = slot < count
    key = jnp.where(live, line, groups) * cap + slot
    rank = jnp.sum((key[None, :] < key[:, None]).astype(jnp.int32), axis=1)
    at = rank[None, :] == slot[:, None]
    order = jnp.sum(jnp.where(at, slot[None, :], 0), axis=1)
    group = jnp.sum(jnp.where(at, jnp.where(live, line, groups)[None, :], 0), axis=1)
    partner = jnp.sum(jnp.where(at, other[None, :], 0), axis=1)
    order = jnp.where(live, order, order[0])
    partner = jnp.where(live, partner, partner[0])
    follows = jnp.concatenate([jnp.zeros((1,), jnp.int32), (group[1:] == group[:-1]).astype(jnp.int32)])
    below = jnp.sum((jnp.where(live, line, groups)[None, :] <= jnp.arange(groups, dtype=jnp.int32)[:, None]).astype(jnp.int32), axis=1)
    member = jnp.sum((jnp.where(live, line, groups)[None, :] == jnp.arange(groups, dtype=jnp.int32)[:, None]).astype(jnp.int32), axis=1)
    last = jnp.maximum(below - 1, 0)
    return order, partner, follows, last, (member > 0).astype(jnp.int32)


def shards(n_row, n_col, block_values, block_index, block_count, strength, raw_scores):
    cap, size = block_values.shape[2], block_values.shape[3]
    seg, rhs, _ = raw_scores.shape
    rows, cols = block_index[0, 0, 0], block_index[0, 0, 1]
    count = block_count[0, 0]
    n_local, n_other = n_col * seg, n_row * seg
    order_r, partner_r, follows_r, last_r, has_r = plan(rows, cols, count, n_local)
    order_c, partner_c, follows_c, last_c, has_c = plan(cols, rows, count, n_other)
    order = jnp.concatenate([order_r, partner_r, order_c, partner_c, last_r, last_c])
    keep = jnp.concatenate([follows_r, follows_c, has_r, has_c]).astype(F32)
    live = (jnp.arange(cap, dtype=jnp.int32) < count).astype(F32)[None, :]
    gain = jnp.broadcast_to(strength[:, None], (rhs, size))
    field = (seg, rhs, size)
    vmem = pl.BlockSpec(memory_space=pltpu.VMEM)
    smem = pl.BlockSpec(memory_space=pltpu.SMEM)
    many = lambda shape: [pltpu.VMEM(shape, F32) for _ in range(ITERS)]
    scratch = [
        pltpu.VMEM((cap, size, size), F32),
        pltpu.VMEM((cap, size, 2 * size), BF16),
        pltpu.VMEM((cap, size, 2 * size), BF16),
        pltpu.VMEM((cap, size), F32),
        pltpu.VMEM((cap, size), F32),
        pltpu.VMEM((cap, rhs, size), F32),
        pltpu.VMEM((8, size), F32),
        pltpu.VMEM((8, size), F32),
        pltpu.VMEM((ITERS,) + field, F32),
        pltpu.VMEM(field, F32),
        pltpu.VMEM(field, F32),
        pltpu.VMEM(field, F32),
    ]
    scratch += many((n_local, rhs, size)) + many((n_other, rhs, size))
    scratch += many((n_local, rhs, size)) + many((n_other, rhs, size))
    scratch += many((n_local, rhs, size)) + many((n_other, rhs, size))
    scratch += many((8, size)) + many((8, size))
    scratch += many((n_col, 8, size)) + many((n_row, 8, size))
    scratch += [
        pltpu.VMEM((n_col, 8, size), F32),
        pltpu.VMEM((n_row, 8, size), F32),
        pltpu.VMEM((n_col, 8, size), F32),
        pltpu.VMEM((n_row, 8, size), F32),
    ]
    most = max(n_row, n_col)
    scratch += [
        pltpu.SemaphoreType.DMA,
        pltpu.SemaphoreType.DMA((6 * ITERS + 2, most)),
        pltpu.SemaphoreType.DMA((6 * ITERS + 2, most)),
    ]
    return pl.pallas_call(
        functools.partial(body, n_row, n_col),
        out_shape=(jax.ShapeDtypeStruct(field, F32), jax.ShapeDtypeStruct(field, F32)),
        in_specs=[pl.BlockSpec(memory_space=pl.ANY), smem, smem, vmem, vmem, vmem, vmem],
        out_specs=(vmem, vmem),
        scratch_shapes=scratch,
        compiler_params=pltpu.CompilerParams(
            collective_id=0, has_side_effects=True, vmem_limit_bytes=56 * 1024 * 1024
        ),
    )(block_values, order, keep, block_index[0, 0], live, gain, raw_scores)


def solution(mesh):
    n_row, n_col = mesh.shape["row"], mesh.shape["col"]
    placed = (
        P("row", "col", None, None, None),
        P("row", "col", None, None),
        P("row", "col"),
        P(),
        P(("row", "col"), None, None),
    )
    return jax.shard_map(
        functools.partial(shards, n_row, n_col),
        mesh=mesh,
        in_specs=placed,
        out_specs=(P(("row", "col"), None, None), P(("row", "col"), None, None)),
        check_vma=False,
    )
```

time: 918 us -> 126 us (0.14)
  blocking collectives: 616 us -> 0 us
  waiting for transfers between devices: 195 us -> 0 us
  Pallas kernels: 0 us -> 116 us
  matrix products: 37.9 us -> 0 us
  other arithmetic: 35.3 us -> 2.82 us
  between operations: 16.3 us -> 1.34 us
  local copies, waits for them, and re-layouts: 15.9 us -> 5.59 us
    psum x5 -> x0, blocking collectives: 380 us -> none  [global_sum(): return lax.psum(partial_sum, ('row', 'col'))]
    reduce_scatter x6 -> x0, waiting for transfers between devices: 195 us -> none  [the longest x3 114 us: fold_terms(): lax.psum_scatter(row_part, 'col', scatter_dimension=0, tiled=True)]
    unnamed x2 -> x0, blocking collectives: 120 us -> none
    all_gather x6 -> x0, blocking collectives: 116 us -> none  [the longest x3 58.3 us: shards(): panel_rows = lax.all_gather(direction, 'col', axis=0, tiled=True)]
    pallas_call x0 -> x1, Pallas kernels: none -> 116 us  [shards(): pl.pallas_call(functools.partial(body, n_row, n_col), out_shape=(jax.Shap...]
    dot_general x8 -> x0, matrix products: 37.9 us -> none  [the longest x4 22 us: local_terms(): jnp.einsum('crk,cik->cri', picked_cols, values, precision=lax.Precision.H...]
    scatter-add x8 -> x0, other arithmetic: 28 us -> none  [the longest x4 15 us: local_terms(): jax.ops.segment_sum(to_cols, col_index, num_segments=panel_cols.shape[0])]
  transfers between devices with their start and end apart: 6 -> 0, of which waited for: 4 -> 0; matrix products, arithmetic and copies ran while one was open for 5% -> 0% of each run, Pallas kernels for 0% -> 0%
where the time goes in v1:
time: 126 us; the launch traced here: 125 us
  Pallas kernels  116 us (92%)
  local copies, waits for them, and re-layouts  5.59 us (4%)
  other arithmetic  2.82 us (2%)
  between operations  1.34 us (1%)
    pallas_call x1, Pallas kernels, shards(): pl.pallas_call(functools.partial(body, n_row, n_col), out_shape=(jax.Shap...  116 us
    unnamed x2, local copies, waits for them, and re-layouts  2.75 us

profile of v1, /device:TPU:1, one launch (start us, length us, event | category | flops | bytes accessed | tf_op | source)
XLA Modules:
  0.0 125.3 jit_solution(14949112799607757903)
XLA Ops:
  1.3 0.5 compare_convert_fusion.live_ref
  1.8 0.8 slice_bitcast_fusion.1
  2.6 0.8 iota_add_fusion
  3.3 0.2 convert_reduce_fusion
  3.5 0.2 convert_reduce_fusion.1
  3.7 0.2 select_reduce_fusion.1
  3.8 0.2 select_reduce_fusion
  4.0 0.1 slice_compare_fusion
  4.1 0.2 convert_reduce_fusion.2
  4.3 0.1 concatenate.10
  4.4 0.6 convert_convert_fusion.keep
  5.0 0.6 concatenate.9.order
  5.7 1.3 %broadcast_in_dim.108.gain_ref = f32[32,128]{1,0:T(8,128)} broadcast(f32[32]{0:T(128)} %param.8), dimensions={0} | broadcast | bytes 16512 | tf_op jit(solution)/shard_map/broadcast_in_dim | solution.py:369
  7.0 115.6 %shard_map.68 = (f32[2,32,128]{2,1,0:T(8,128)}, f32[2,32,128]{2,1,0:T(8,128)}) custom-call(f32[1,1,40,128,128]{4,3,2,1,0:T(8,128)} %values_hbm.1, s32[224]{0:T(256)} %concatenate.9.order, f32[144]{0:T(256)} %convert_convert_fusion.keep, s32[2,40]{1,0:T(2,128)} %bitcast.24, f32[1,40]{1,0:T(1,128)} %compare_convert_fusion.live_ref, ...), custom_call_target="tpu_custom_call" | custom-call | tf_op jit(solution)/shard_map/pallas_call | solution.py:405
  122.5 1.4 %copy.10 = f32[2,32,128]{2,1,0:T(8,128)} copy(f32[2,32,128]{2,1,0:T(8,128)} %get-tuple-element.30) | data formatting | bytes 65536
  123.9 1.4 %copy.11 = f32[2,32,128]{2,1,0:T(8,128)} copy(f32[2,32,128]{2,1,0:T(8,128)} %get-tuple-element.31) | data formatting | bytes 65536
  (6 shorter events, 0.1 us)

commit v2 on v1

v2 whole, which is shorter than its diff:
```python
import functools

import jax
import jax.numpy as jnp
from jax import lax
from jax.experimental import pallas as pl
from jax.experimental.pallas import tpu as pltpu
from jax.sharding import PartitionSpec as P

ITERS = 3
MESH = pl.DeviceIdType.MESH
F32 = jnp.float32
BF16 = jnp.bfloat16


def split(x):
    high = x.astype(BF16)
    low = (x - high.astype(F32)).astype(BF16)
    return high, low


def product(field, weights):
    size = field.shape[0]
    width = field.shape[1]
    high, low = split(field)
    both = jnp.concatenate([high, low], axis=0)
    out = jnp.dot(both, weights, preferred_element_type=F32)
    upper = out[:size, :width]
    return upper + ((out[size:, :width] + out[:size, width:]) + out[size:, width:])


def body(
    n_row,
    n_col,
    values_hbm,
    order,
    keep,
    index_ref,
    live_ref,
    gain_ref,
    raw_ref,
    smooth_ref,
    resid_ref,
    *scratch,
):
    names = iter(scratch)
    take = lambda: next(names)
    each_step = lambda: [take() for _ in range(ITERS)]
    stored, natural, turned, sums_row, sums_col = take(), take(), take(), take(), take()
    running, resid, degree, direct, image = take(), take(), take(), take(), take()
    panel_rows, panel_cols = each_step(), each_step()
    row_send, col_send = each_step(), each_step()
    swap_got, row_sum = each_step(), each_step()
    row_got, col_got = each_step(), each_step()
    dot_own, dot_line = each_step(), each_step()
    dot_col_got, dot_row_got = each_step(), each_step()
    deg_row_send, deg_col_send, deg_row_got, deg_col_got = take(), take(), take(), take()
    value_sem, sent, got = take(), take(), take()

    a = lax.axis_index("row")
    c = lax.axis_index("col")
    core = lax.rem(c, 2)
    chip = c // 2
    sibling = c + 1 - 2 * core
    n_chip = n_col // 2
    far = sorted(range(1, n_chip), key=lambda k: -min(k, n_chip - k))
    cap = stored.shape[0]
    size = stored.shape[1]
    seg = raw_ref.shape[0]
    rhs = raw_ref.shape[1]
    n_local = n_col * seg
    n_other = n_row * seg
    GATHER_COL, GATHER_ROW, SWAP, PART_COL, PART_ROW, DOT_COL, DOT_ROW = range(7)
    KINDS = 7
    DEG_COL, DEG_ROW = KINDS * ITERS, KINDS * ITERS + 1

    fetch = pltpu.make_async_copy(values_hbm.at[0, 0], stored, value_sem)
    fetch.start()

    barrier = pltpu.get_barrier_semaphore()

    def greet_col(k, _):
        pl.semaphore_signal(
            barrier, inc=1, device_id=(a, lax.rem(c + k, n_col)), device_id_type=MESH
        )
        return 0

    def greet_row(k, _):
        pl.semaphore_signal(
            barrier, inc=1, device_id=(lax.rem(a + k, n_row), c), device_id_type=MESH
        )
        return 0

    lax.fori_loop(1, n_col, greet_col, 0)
    lax.fori_loop(1, n_row, greet_row, 0)
    resid[0] = raw_ref[...]
    panel_rows[0][pl.ds(seg * c, seg)] = raw_ref[...]
    panel_cols[0][pl.ds(seg * a, seg)] = raw_ref[...]
    pl.semaphore_wait(barrier, n_col + n_row - 2)

    def send(src, dst, target, which, out_slot, in_slot):
        pltpu.make_async_remote_copy(
            src_ref=src,
            dst_ref=dst,
            send_sem=sent.at[which, out_slot],
            recv_sem=got.at[which, in_slot],
            device_id=target,
            device_id_type=MESH,
        ).start()

    def each_col(act):
        lax.fori_loop(1, n_col, lambda k, _: (act(lax.rem(c + k, n_col)), 0)[1], 0)

    def each_row(act):
        lax.fori_loop(1, n_row, lambda k, _: (act(lax.rem(a + k, n_row)), 0)[1], 0)

    def rows_below(act):
        lax.fori_loop(0, a, lambda k, _: (act(k), 0)[1], 0)

    def rows_above(act):
        lax.fori_loop(a + 1, n_row, lambda k, _: (act(k), 0)[1], 0)

    def other_chips(act):
        for k in far:
            act(lax.rem(chip + k, n_chip))

    def arrive(dst, which, slot):
        pltpu.make_async_copy(dst, dst, got.at[which, slot]).wait()

    def leave(src, which, slot):
        pltpu.make_async_copy(src, src, sent.at[which, slot]).wait()

    def gather(step):
        where = panel_rows[step].at[pl.ds(seg * c, seg)]
        kind = KINDS * step + GATHER_COL
        other_chips(lambda z: send(resid.at[step], where, (a, 2 * z + core), kind, 0, c))
        send(resid.at[step], where, (a, sibling), kind, 0, c)
        where_col = panel_cols[step].at[pl.ds(seg * a, seg)]
        rows_below(lambda r: send(resid.at[step], where_col, (r, c), kind + GATHER_ROW, r, a))

    def pass_on(step):
        kind = KINDS * step + GATHER_COL
        for k in reversed(far):
            z = lax.rem(chip + k, n_chip)
            piece = panel_rows[step].at[pl.ds(seg * (2 * z + core), seg)]
            arrive(piece, kind, 2 * z + core)
            send(piece, piece, (a, sibling), kind, 1, 2 * z + core)

    def from_sibling(step):
        kind = KINDS * step + GATHER_COL
        for k in [0] + far[::-1]:
            z = lax.rem(chip + k, n_chip)
            slot = 2 * z + 1 - core
            arrive(panel_rows[step].at[pl.ds(seg * slot, seg)], kind, slot)

    def sends_done(step):
        kind = KINDS * step
        some = lambda ref, count: ref.at[pl.ds(0, count)]
        leave(some(panel_rows[step], seg * n_chip), kind + GATHER_COL, 0)
        leave(some(panel_rows[step], seg * (n_chip - 1)), kind + GATHER_COL, 1)
        rows_below(lambda r: leave(resid.at[step], kind + GATHER_ROW, r))
        leave(row_send[step].at[0], kind + SWAP, 0)
        leave(some(row_sum[step], seg * (n_chip - 1)), kind + PART_COL, 0)
        rows_above(lambda r: leave(some(col_send[step], seg), kind + PART_ROW, r))
        leave(some(dot_col_got[step], n_col - 1), kind + DOT_COL, 0)
        leave(some(dot_row_got[step], n_row - 1), kind + DOT_ROW, 0)

    gather(0)
    fetch.wait()

    def prepare(q, _):
        block = stored[q]
        flipped = block.T
        high, low = split(block)
        natural[q, :, :size] = high
        natural[q, :, size:] = low
        high, low = split(flipped)
        turned[q, :, :size] = high
        turned[q, :, size:] = low
        sums_row[pl.ds(q, 1), :] = jnp.sum(flipped, axis=0, keepdims=True)
        sums_col[pl.ds(q, 1), :] = jnp.sum(block, axis=0, keepdims=True)
        return 0

    lax.fori_loop(0, cap, prepare, 0, unroll=2)

    live = live_ref[...]

    def pick(line, count):
        wanted = lax.broadcasted_iota(jnp.int32, (count, cap), 0)
        return jnp.where(wanted == index_ref[line : line + 1, :], live, 0.0)

    degree_rows = jnp.dot(
        pick(0, n_local), sums_row[...], precision=lax.Precision.HIGHEST, preferred_element_type=F32
    )
    degree_cols = jnp.dot(
        pick(1, n_other), sums_col[...], precision=lax.Precision.HIGHEST, preferred_element_type=F32
    )
    for peer in range(n_col):
        deg_row_send[peer] = degree_rows[seg * peer : seg * peer + seg, :]
    for peer in range(n_row):
        deg_col_send[peer] = degree_cols[seg * peer : seg * peer + seg, :]
    each_col(lambda p: send(deg_row_send.at[p], deg_row_got.at[c], (a, p), DEG_COL, 0, 0))
    rows_above(lambda r: send(deg_col_send.at[r], deg_col_got.at[a], (r, c), DEG_ROW, r, a))
    deg_row_got[c] = deg_row_send[c]
    deg_col_got[a] = deg_col_send[a]

    gains = gain_ref[...]

    def pass_over(weights, panel, base, limit):
        def slot(k, total):
            weight = weights[order[base + k]]
            field = panel[order[base + cap + k]]
            total = total * keep[limit + k] + product(field, weight)
            running[k] = total
            return total

        lax.fori_loop(0, cap, slot, jnp.zeros((rhs, size), F32), unroll=4)

    def total_of(ref, count):
        out = ref[0]
        for k in range(1, count):
            out = out + ref[k]
        return out

    def dense_row(c_of):
        return (c_of % 2, (c_of // 2) * seg)

    gamma_old = None
    alpha_old = None
    for step in range(ITERS):
        kind = KINDS * step
        if step > 0:
            sends_done(step - 1)
        rows_above(lambda r: arrive(panel_cols[step].at[pl.ds(seg * r, seg)], kind + GATHER_ROW, r))
        pass_over(turned, panel_cols[step], 0, 0)
        for k in far + [0]:
            z = lax.rem(chip + k, n_chip)
            for half in range(2):
                for j in range(seg):
                    u = seg * (2 * z + half) + j
                    row_send[step][half, seg * z + j] = (
                        running[order[4 * cap + u]] * keep[2 * cap + u]
                    )
            piece = pl.ds(seg * z, seg)
            send(
                row_send[step].at[1 - core, piece],
                swap_got[step].at[piece],
                (a, sibling),
                kind + SWAP,
                0,
                z,
            )
        for k in far + [0]:
            z = lax.rem(chip + k, n_chip)
            piece = pl.ds(seg * z, seg)
            arrive(swap_got[step].at[piece], kind + SWAP, z)
            for j in range(seg):
                row_sum[step][seg * z + j] = row_send[step][core, seg * z + j] + swap_got[step][seg * z + j]
            if k:
                send(
                    row_sum[step].at[piece],
                    row_got[step].at[pl.ds(seg * chip, seg)],
                    (a, 2 * z + core),
                    kind + PART_COL,
                    0,
                    chip,
                )
        pass_on(step)
        from_sibling(step)
        if step == 0:
            arrive(deg_row_got.at[pl.ds(0, n_col - 1)], DEG_COL, 0)
            rows_below(lambda r: arrive(deg_col_got.at[r], DEG_ROW, r))
            here = total_of(deg_row_got, n_col)
            here = here + lax.fori_loop(
                0, a + 1, lambda k, t: t + deg_col_got[k], jnp.zeros_like(here)
            )
            for j in range(seg):
                degree[j] = jnp.broadcast_to(here[j : j + 1, :], (rhs, size))
        own = resid[step]
        square = own * own
        cross = None
        for u in range(n_local):
            half, first = dense_row(u // seg)
            term = panel_rows[step][u] * row_send[step][half, first + u % seg]
            cross = term if cross is None else cross + term
        gamma_part = square[0]
        delta_part = degree[0] * square[0]
        for j in range(1, seg):
            gamma_part = gamma_part + square[j]
            delta_part = delta_part + degree[j] * square[j]
        delta_part = gamma_part + gains * (delta_part - 2.0 * cross)
        parts = jnp.concatenate([gamma_part, delta_part, jnp.zeros((size - 2 * rhs, size), F32)], axis=0)
        dot_own[step][...] = jnp.sum(parts.T, axis=0, keepdims=True)
        each_row(lambda r: send(dot_own[step], dot_row_got[step].at[a], (r, c), kind + DOT_ROW, 0, 0))
        dot_row_got[step][a] = dot_own[step][...]

        pass_over(natural, panel_rows[step], 2 * cap, cap)
        for v in range(n_other):
            col_send[step][v] = running[order[4 * cap + n_local + v]] * keep[2 * cap + n_local + v]
        rows_above(
            lambda r: send(
                col_send[step].at[pl.ds(seg * r, seg)],
                col_got[step].at[pl.ds(seg * a, seg)],
                (r, c),
                kind + PART_ROW,
                r,
                a,
            )
        )
        col_got[step][pl.ds(seg * a, seg)] = col_send[step][pl.ds(seg * a, seg)]

        arrive(dot_row_got[step].at[pl.ds(0, n_row - 1)], kind + DOT_ROW, 0)
        dot_line[step][...] = total_of(dot_row_got[step], n_row)
        each_col(lambda p: send(dot_line[step], dot_col_got[step].at[c], (a, p), kind + DOT_COL, 0, 0))
        dot_col_got[step][c] = dot_line[step][...]

        rows_below(lambda r: arrive(col_got[step].at[pl.ds(seg * r, seg)], kind + PART_ROW, r))

        def add_cols(k, both):
            return tuple(both[j] + col_got[step][seg * k + j] for j in range(seg))

        spread = lax.fori_loop(
            0, a + 1, add_cols, tuple(row_sum[step][seg * chip + j] for j in range(seg))
        )
        spread = list(spread)
        for k in far[::-1]:
            z = lax.rem(chip + k, n_chip)
            arrive(row_got[step].at[pl.ds(seg * z, seg)], kind + PART_COL, z)
            for j in range(seg):
                spread[j] = spread[j] + row_got[step][seg * z + j]

        arrive(dot_col_got[step].at[pl.ds(0, n_col - 1)], kind + DOT_COL, 0)
        dots = total_of(dot_col_got[step], n_col)
        dots = jnp.broadcast_to(dots, (size, size)).T
        gamma = dots[:rhs]
        delta = dots[rhs : 2 * rhs]
        if step == 0:
            alpha = gamma / delta
            beta = None
        else:
            beta = gamma / gamma_old
            alpha = gamma / (delta - beta * gamma / alpha_old)
        for j in range(seg):
            r = own[j]
            w = r + gains * (degree[j] * r - spread[j])
            if step == 0:
                d, ad = r, w
                x = alpha * d
            else:
                d = r + beta * direct[j]
                ad = w + beta * image[j]
                x = smooth_ref[j] + alpha * d
            nxt = r - alpha * ad
            smooth_ref[j] = x
            if step < ITERS - 1:
                direct[j] = d
                image[j] = ad
                resid[step + 1, j] = nxt
            else:
                resid_ref[j] = nxt
        if step < ITERS - 1:
            gather(step + 1)
            panel_rows[step + 1][pl.ds(seg * c, seg)] = resid[step + 1]
            panel_cols[step + 1][pl.ds(seg * a, seg)] = resid[step + 1]
        gamma_old, alpha_old = gamma, alpha

    sends_done(ITERS - 1)
    leave(deg_row_got.at[pl.ds(0, n_col - 1)], DEG_COL, 0)
    rows_above(lambda r: leave(deg_col_send.at[r], DEG_ROW, r))


def plan(line, other, count, groups):
    cap = line.shape[0]
    slot = jnp.arange(cap, dtype=jnp.int32)
    live = slot < count
    key = jnp.where(live, line, groups) * cap + slot
    rank = jnp.sum((key[None, :] < key[:, None]).astype(jnp.int32), axis=1)
    at = rank[None, :] == slot[:, None]
    order = jnp.sum(jnp.where(at, slot[None, :], 0), axis=1)
    group = jnp.sum(jnp.where(at, jnp.where(live, line, groups)[None, :], 0), axis=1)
    partner = jnp.sum(jnp.where(at, other[None, :], 0), axis=1)
    order = jnp.where(live, order, order[0])
    partner = jnp.where(live, partner, partner[0])
    follows = jnp.concatenate([jnp.zeros((1,), jnp.int32), (group[1:] == group[:-1]).astype(jnp.int32)])
    below = jnp.sum((jnp.where(live, line, groups)[None, :] <= jnp.arange(groups, dtype=jnp.int32)[:, None]).astype(jnp.int32), axis=1)
    member = jnp.sum((jnp.where(live, line, groups)[None, :] == jnp.arange(groups, dtype=jnp.int32)[:, None]).astype(jnp.int32), axis=1)
    last = jnp.maximum(below - 1, 0)
    return order, partner, follows, last, (member > 0).astype(jnp.int32)


def shards(n_row, n_col, block_values, block_index, block_count, strength, raw_scores):
    cap, size = block_values.shape[2], block_values.shape[3]
    seg, rhs, _ = raw_scores.shape
    rows, cols = block_index[0, 0, 0], block_index[0, 0, 1]
    count = block_count[0, 0]
    n_local, n_other = n_col * seg, n_row * seg
    order_r, partner_r, follows_r, last_r, has_r = plan(rows, cols, count, n_local)
    order_c, partner_c, follows_c, last_c, has_c = plan(cols, rows, count, n_other)
    order = jnp.concatenate([order_r, partner_r, order_c, partner_c, last_r, last_c])
    keep = jnp.concatenate([follows_r, follows_c, has_r, has_c]).astype(F32)
    live = (jnp.arange(cap, dtype=jnp.int32) < count).astype(F32)[None, :]
    gain = jnp.broadcast_to(strength[:, None], (rhs, size))
    field = (seg, rhs, size)
    vmem = pl.BlockSpec(memory_space=pltpu.VMEM)
    smem = pl.BlockSpec(memory_space=pltpu.SMEM)
    many = lambda shape: [pltpu.VMEM(shape, F32) for _ in range(ITERS)]
    n_chip = n_col // 2
    scratch = [
        pltpu.VMEM((cap, size, size), F32),
        pltpu.VMEM((cap, size, 2 * size), BF16),
        pltpu.VMEM((cap, size, 2 * size), BF16),
        pltpu.VMEM((cap, size), F32),
        pltpu.VMEM((cap, size), F32),
        pltpu.VMEM((cap, rhs, size), F32),
        pltpu.VMEM((ITERS,) + field, F32),
        pltpu.VMEM(field, F32),
        pltpu.VMEM(field, F32),
        pltpu.VMEM(field, F32),
    ]
    scratch += many((n_local, rhs, size)) + many((n_other, rhs, size))
    scratch += many((2, n_chip * seg, rhs, size)) + many((n_other, rhs, size))
    scratch += many((n_chip * seg, rhs, size)) + many((n_chip * seg, rhs, size))
    scratch += many((n_chip * seg, rhs, size)) + many((n_other, rhs, size))
    scratch += many((1, size)) + many((1, size))
    scratch += many((n_col, 1, size)) + many((n_row, 1, size))
    scratch += [
        pltpu.VMEM((n_col, seg, size), F32),
        pltpu.VMEM((n_row, seg, size), F32),
        pltpu.VMEM((n_col, seg, size), F32),
        pltpu.VMEM((n_row, seg, size), F32),
    ]
    most = max(n_row, n_col)
    scratch += [
        pltpu.SemaphoreType.DMA,
        pltpu.SemaphoreType.DMA((7 * ITERS + 2, most)),
        pltpu.SemaphoreType.DMA((7 * ITERS + 2, most)),
    ]
    return pl.pallas_call(
        functools.partial(body, n_row, n_col),
        out_shape=(jax.ShapeDtypeStruct(field, F32), jax.ShapeDtypeStruct(field, F32)),
        in_specs=[pl.BlockSpec(memory_space=pl.ANY), smem, smem, vmem, vmem, vmem, vmem],
        out_specs=(vmem, vmem),
        scratch_shapes=scratch,
        compiler_params=pltpu.CompilerParams(
            collective_id=0, has_side_effects=True, vmem_limit_bytes=56 * 1024 * 1024
        ),
    )(block_values, order, keep, block_index[0, 0], live, gain, raw_scores)


def solution(mesh):
    n_row, n_col = mesh.shape["row"], mesh.shape["col"]
    placed = (
        P("row", "col", None, None, None),
        P("row", "col", None, None),
        P("row", "col"),
        P(),
        P(("row", "col"), None, None),
    )
    return jax.shard_map(
        functools.partial(shards, n_row, n_col),
        mesh=mesh,
        in_specs=placed,
        out_specs=(P(("row", "col"), None, None), P(("row", "col"), None, None)),
        check_vma=False,
    )
```

time: 126 us -> 96.7 us (0.77)
  Pallas kernels: 116 us -> 86.6 us
    pallas_call x1, Pallas kernels: 116 us -> 86.6 us  [shards(): pl.pallas_call(functools.partial(body, n_row, n_col), out_shape=(jax.Shap...]
where the time goes in v2:
time: 96.7 us; the launch traced here: 96.4 us
  Pallas kernels  86.6 us (90%)
  local copies, waits for them, and re-layouts  5.59 us (6%)
  other arithmetic  2.82 us (3%)
  between operations  1.34 us (1%)
    pallas_call x1, Pallas kernels, shards(): pl.pallas_call(functools.partial(body, n_row, n_col), out_shape=(jax.Shap...  86.6 us
    unnamed x2, local copies, waits for them, and re-layouts  2.75 us

profile of v2, /device:TPU:1, one launch (start us, length us, event | category | flops | bytes accessed | tf_op | source)
XLA Modules:
  0.0 96.4 jit_solution(17800676124815359037)
XLA Ops:
  1.3 0.5 compare_convert_fusion.live_ref
  1.8 0.8 slice_bitcast_fusion.1
  2.6 0.8 iota_add_fusion
  3.3 0.2 convert_reduce_fusion
  3.5 0.2 convert_reduce_fusion.1
  3.7 0.2 select_reduce_fusion.1
  3.8 0.2 select_reduce_fusion
  4.0 0.1 slice_compare_fusion
  4.1 0.2 convert_reduce_fusion.2
  4.3 0.1 concatenate.10
  4.4 0.6 convert_convert_fusion.keep
  5.0 0.6 concatenate.9.order
  5.7 1.3 %broadcast_in_dim.108.gain_ref = f32[32,128]{1,0:T(8,128)} broadcast(f32[32]{0:T(128)} %param.8), dimensions={0} | broadcast | bytes 16512 | tf_op jit(solution)/shard_map/broadcast_in_dim | solution.py:402
  7.0 86.6 %shard_map.68 = (f32[2,32,128]{2,1,0:T(8,128)}, f32[2,32,128]{2,1,0:T(8,128)}) custom-call(f32[1,1,40,128,128]{4,3,2,1,0:T(8,128)} %values_hbm.1, s32[224]{0:T(256)} %concatenate.9.order, f32[144]{0:T(256)} %convert_convert_fusion.keep, s32[2,40]{1,0:T(2,128)} %bitcast.24, f32[1,40]{1,0:T(1,128)} %compare_convert_fusion.live_ref, ...), custom_call_target="tpu_custom_call" | custom-call | tf_op jit(solution)/shard_map/pallas_call | solution.py:438
  93.6 1.4 %copy.10 = f32[2,32,128]{2,1,0:T(8,128)} copy(f32[2,32,128]{2,1,0:T(8,128)} %get-tuple-element.30) | data formatting | bytes 65536
  95.0 1.4 %copy.11 = f32[2,32,128]{2,1,0:T(8,128)} copy(f32[2,32,128]{2,1,0:T(8,128)} %get-tuple-element.31) | data formatting | bytes 65536
  (6 shorter events, 0.1 us)

commit v3 on v2

--- a/solution.py
+++ b/solution.py
@@ -33,11 +33,9 @@
     n_row,
     n_col,
     values_hbm,
-    order,
-    keep,
     index_ref,
-    live_ref,
-    gain_ref,
+    count_ref,
+    strength_ref,
     raw_ref,
     smooth_ref,
     resid_ref,
@@ -55,7 +53,8 @@
     dot_own, dot_line = each_step(), each_step()
     dot_col_got, dot_row_got = each_step(), each_step()
     deg_row_send, deg_col_send, deg_row_got, deg_col_got = take(), take(), take(), take()
-    value_sem, sent, got = take(), take(), take()
+    gain_ref, listed, slots, scales, slots_at, scales_at = [take() for _ in range(6)]
+    value_sem, plan_sem, sent, got = take(), take(), take(), take()
 
     a = lax.axis_index("row")
     c = lax.axis_index("col")
@@ -96,76 +95,13 @@
     resid[0] = raw_ref[...]
     panel_rows[0][pl.ds(seg * c, seg)] = raw_ref[...]
     panel_cols[0][pl.ds(seg * a, seg)] = raw_ref[...]
-    pl.semaphore_wait(barrier, n_col + n_row - 2)
-
-    def send(src, dst, target, which, out_slot, in_slot):
-        pltpu.make_async_remote_copy(
-            src_ref=src,
-            dst_ref=dst,
-            send_sem=sent.at[which, out_slot],
-            recv_sem=got.at[which, in_slot],
-            device_id=target,
-            device_id_type=MESH,
-        ).start()
-
-    def each_col(act):
-        lax.fori_loop(1, n_col, lambda k, _: (act(lax.rem(c + k, n_col)), 0)[1], 0)
-
-    def each_row(act):
-        lax.fori_loop(1, n_row, lambda k, _: (act(lax.rem(a + k, n_row)), 0)[1], 0)
-
-    def rows_below(act):
-        lax.fori_loop(0, a, lambda k, _: (act(k), 0)[1], 0)
-
-    def rows_above(act):
-        lax.fori_loop(a + 1, n_row, lambda k, _: (act(k), 0)[1], 0)
-
-    def other_chips(act):
-        for k in far:
-            act(lax.rem(chip + k, n_chip))
-
-    def arrive(dst, which, slot):
-        pltpu.make_async_copy(dst, dst, got.at[which, slot]).wait()
-
-    def leave(src, which, slot):
-        pltpu.make_async_copy(src, src, sent.at[which, slot]).wait()
-
-    def gather(step):
-        where = panel_rows[step].at[pl.ds(seg * c, seg)]
-        kind = KINDS * step + GATHER_COL
-        other_chips(lambda z: send(resid.at[step], where, (a, 2 * z + core), kind, 0, c))
-        send(resid.at[step], where, (a, sibling), kind, 0, c)
-        where_col = panel_cols[step].at[pl.ds(seg * a, seg)]
-        rows_below(lambda r: send(resid.at[step], where_col, (r, c), kind + GATHER_ROW, r, a))
-
-    def pass_on(step):
-        kind = KINDS * step + GATHER_COL
-        for k in reversed(far):
-            z = lax.rem(chip + k, n_chip)
-            piece = panel_rows[step].at[pl.ds(seg * (2 * z + core), seg)]
-            arrive(piece, kind, 2 * z + core)
-            send(piece, piece, (a, sibling), kind, 1, 2 * z + core)
-
-    def from_sibling(step):
-        kind = KINDS * step + GATHER_COL
-        for k in [0] + far[::-1]:
-            z = lax.rem(chip + k, n_chip)
-            slot = 2 * z + 1 - core
-            arrive(panel_rows[step].at[pl.ds(seg * slot, seg)], kind, slot)
-
-    def sends_done(step):
-        kind = KINDS * step
-        some = lambda ref, count: ref.at[pl.ds(0, count)]
-        leave(some(panel_rows[step], seg * n_chip), kind + GATHER_COL, 0)
-        leave(some(panel_rows[step], seg * (n_chip - 1)), kind + GATHER_COL, 1)
-        rows_below(lambda r: leave(resid.at[step], kind + GATHER_ROW, r))
-        leave(row_send[step].at[0], kind + SWAP, 0)
-        leave(some(row_sum[step], seg * (n_chip - 1)), kind + PART_COL, 0)
-        rows_above(lambda r: leave(some(col_send[step], seg), kind + PART_ROW, r))
-        leave(some(dot_col_got[step], n_col - 1), kind + DOT_COL, 0)
-        leave(some(dot_row_got[step], n_row - 1), kind + DOT_ROW, 0)
-
-    gather(0)
+    make_plan(index_ref, count_ref[...], cap, n_local, n_other, listed, slots, scales)
+    to_slots = pltpu.make_async_copy(slots, slots_at, plan_sem.at[0])
+    to_scales = pltpu.make_async_copy(scales, scales_at, plan_sem.at[1])
+    to_slots.start()
+    to_scales.start()
+    for s in range(rhs):
+        gain_ref[s : s + 1, :] = jnp.full((1, size), strength_ref[s], F32)
     fetch.wait()
 
     def prepare(q, _):
@@ -181,13 +117,86 @@
         sums_col[pl.ds(q, 1), :] = jnp.sum(block, axis=0, keepdims=True)
         return 0
 
-    lax.fori_loop(0, cap, prepare, 0, unroll=2)
-
-    live = live_ref[...]
+    lax.fori_loop(0, cap // 2, prepare, 0, unroll=2)
+    pl.semaphore_wait(barrier, n_col + n_row - 2)
+
+    def send(src, dst, target, which, out_slot, in_slot):
+        pltpu.make_async_remote_copy(
+            src_ref=src,
+            dst_ref=dst,
+            send_sem=sent.at[which, out_slot],
+            recv_sem=got.at[which, in_slot],
+            device_id=target,
+            device_id_type=MESH,
+        ).start()
+
+    def each_col(act):
+        lax.fori_loop(1, n_col, lambda k, _: (act(lax.rem(c + k, n_col)), 0)[1], 0)
+
+    def each_row(act):
+        lax.fori_loop(1, n_row, lambda k, _: (act(lax.rem(a + k, n_row)), 0)[1], 0)
+
+    def rows_below(act):
+        lax.fori_loop(0, a, lambda k, _: (act(k), 0)[1], 0)
+
+    def rows_above(act):
+        lax.fori_loop(a + 1, n_row, lambda k, _: (act(k), 0)[1], 0)
+
+    def other_chips(act):
+        for k in far:
+            act(lax.rem(chip + k, n_chip))
+
+    def arrive(dst, which, slot):
+        pltpu.make_async_copy(dst, dst, got.at[which, slot]).wait()
+
+    def leave(src, which, slot):
+        pltpu.make_async_copy(src, src, sent.at[which, slot]).wait()
+
+    def gather(step):
+        where = panel_rows[step].at[pl.ds(seg * c, seg)]
+        kind = KINDS * step + GATHER_COL
+        other_chips(lambda z: send(resid.at[step], where, (a, 2 * z + core), kind, 0, c))
+        send(resid.at[step], where, (a, sibling), kind, 0, c)
+        where_col = panel_cols[step].at[pl.ds(seg * a, seg)]
+        rows_below(lambda r: send(resid.at[step], where_col, (r, c), kind + GATHER_ROW, r, a))
+
+    def pass_on(step):
+        kind = KINDS * step + GATHER_COL
+        for k in reversed(far):
+            z = lax.rem(chip + k, n_chip)
+            piece = panel_rows[step].at[pl.ds(seg * (2 * z + core), seg)]
+            arrive(piece, kind, 2 * z + core)
+            send(piece, piece, (a, sibling), kind, 1, 2 * z + core)
+
+    def from_sibling(step):
+        kind = KINDS * step + GATHER_COL
+        for k in [0] + far[::-1]:
+            z = lax.rem(chip + k, n_chip)
+            slot = 2 * z + 1 - core
+            arrive(panel_rows[step].at[pl.ds(seg * slot, seg)], kind, slot)
+
+    def sends_done(step):
+        kind = KINDS * step
+        some = lambda ref, count: ref.at[pl.ds(0, count)]
+        leave(some(panel_rows[step], seg * n_chip), kind + GATHER_COL, 0)
+        leave(some(panel_rows[step], seg * (n_chip - 1)), kind + GATHER_COL, 1)
+        rows_below(lambda r: leave(resid.at[step], kind + GATHER_ROW, r))
+        leave(row_send[step].at[0], kind + SWAP, 0)
+        leave(some(row_sum[step], seg * (n_chip - 1)), kind + PART_COL, 0)
+        rows_above(lambda r: leave(some(col_send[step], seg), kind + PART_ROW, r))
+        leave(some(dot_col_got[step], n_col - 1), kind + DOT_COL, 0)
+        leave(some(dot_row_got[step], n_row - 1), kind + DOT_ROW, 0)
+
+    gather(0)
+
+    lax.fori_loop(cap // 2, cap, prepare, 0, unroll=2)
+
+    live = lax.broadcasted_iota(jnp.int32, (1, cap), 1) < count_ref[...]
 
     def pick(line, count):
         wanted = lax.broadcasted_iota(jnp.int32, (count, cap), 0)
-        return jnp.where(wanted == index_ref[line : line + 1, :], live, 0.0)
+        chosen = (wanted == index_ref[0, 0, line : line + 1, :]) & live
+        return jnp.where(chosen, 1.0, 0.0)
 
     degree_rows = jnp.dot(
         pick(0, n_local), sums_row[...], precision=lax.Precision.HIGHEST, preferred_element_type=F32
@@ -205,12 +214,14 @@
     deg_col_got[a] = deg_col_send[a]
 
     gains = gain_ref[...]
-
-    def pass_over(weights, panel, base, limit):
+    to_slots.wait()
+    to_scales.wait()
+
+    def pass_over(weights, panel, side):
         def slot(k, total):
-            weight = weights[order[base + k]]
-            field = panel[order[base + cap + k]]
-            total = total * keep[limit + k] + product(field, weight)
+            weight = weights[slots_at[3 * side, k]]
+            field = panel[slots_at[3 * side + 1, k]]
+            total = total * scales_at[2 * side, k] + product(field, weight)
             running[k] = total
             return total
 
@@ -232,14 +243,14 @@
         if step > 0:
             sends_done(step - 1)
         rows_above(lambda r: arrive(panel_cols[step].at[pl.ds(seg * r, seg)], kind + GATHER_ROW, r))
-        pass_over(turned, panel_cols[step], 0, 0)
+        pass_over(turned, panel_cols[step], 0)
         for k in far + [0]:
             z = lax.rem(chip + k, n_chip)
             for half in range(2):
                 for j in range(seg):
                     u = seg * (2 * z + half) + j
                     row_send[step][half, seg * z + j] = (
-                        running[order[4 * cap + u]] * keep[2 * cap + u]
+                        running[slots_at[2, u]] * scales_at[1, u]
                     )
             piece = pl.ds(seg * z, seg)
             send(
@@ -294,9 +305,9 @@
         each_row(lambda r: send(dot_own[step], dot_row_got[step].at[a], (r, c), kind + DOT_ROW, 0, 0))
         dot_row_got[step][a] = dot_own[step][...]
 
-        pass_over(natural, panel_rows[step], 2 * cap, cap)
+        pass_over(natural, panel_rows[step], 1)
         for v in range(n_other):
-            col_send[step][v] = running[order[4 * cap + n_local + v]] * keep[2 * cap + n_local + v]
+            col_send[step][v] = running[slots_at[5, v]] * scales_at[3, v]
         rows_above(
             lambda r: send(
                 col_send[step].at[pl.ds(seg * r, seg)],
@@ -369,37 +380,37 @@
     rows_above(lambda r: leave(deg_col_send.at[r], DEG_ROW, r))
 
 
-def plan(line, other, count, groups):
-    cap = line.shape[0]
-    slot = jnp.arange(cap, dtype=jnp.int32)
-    live = slot < count
-    key = jnp.where(live, line, groups) * cap + slot
-    rank = jnp.sum((key[None, :] < key[:, None]).astype(jnp.int32), axis=1)
-    at = rank[None, :] == slot[:, None]
-    order = jnp.sum(jnp.where(at, slot[None, :], 0), axis=1)
-    group = jnp.sum(jnp.where(at, jnp.where(live, line, groups)[None, :], 0), axis=1)
-    partner = jnp.sum(jnp.where(at, other[None, :], 0), axis=1)
-    order = jnp.where(live, order, order[0])
-    partner = jnp.where(live, partner, partner[0])
-    follows = jnp.concatenate([jnp.zeros((1,), jnp.int32), (group[1:] == group[:-1]).astype(jnp.int32)])
-    below = jnp.sum((jnp.where(live, line, groups)[None, :] <= jnp.arange(groups, dtype=jnp.int32)[:, None]).astype(jnp.int32), axis=1)
-    member = jnp.sum((jnp.where(live, line, groups)[None, :] == jnp.arange(groups, dtype=jnp.int32)[:, None]).astype(jnp.int32), axis=1)
-    last = jnp.maximum(below - 1, 0)
-    return order, partner, follows, last, (member > 0).astype(jnp.int32)
+def make_plan(index_ref, count, cap, n_local, n_other, listed, slots, scales):
+    width = listed.shape[1]
+    listed[...] = jnp.zeros_like(listed)
+    listed[0:2, 0:cap] = index_ref[0, 0]
+    down = lax.broadcasted_iota(jnp.int32, (width, width), 0)
+    across = lax.broadcasted_iota(jnp.int32, (width, width), 1)
+    lines = [jnp.broadcast_to(listed[j : j + 1, :], (width, width)) for j in range(2)]
+    turned = [line.T for line in lines]
+    for side, groups in enumerate((n_local, n_other)):
+        key = jnp.where(across < count, lines[side], groups) * width + across
+        group = jnp.where(down < count, turned[side], groups)
+        key_down = group * width + down
+        rank = jnp.sum(jnp.where(key < key_down, 1, 0), axis=1, keepdims=True)
+        at = rank == across
+        total = lambda x: jnp.sum(x, axis=0, keepdims=True)
+        ordered = total(jnp.where(at, group, 0))
+        before = pltpu.roll(ordered, 1, 1)
+        first = across[0:1, :] == 0
+        below = total(jnp.where(group <= across, 1, 0))
+        member = total(jnp.where(group == across, 1, 0))
+        slots[3 * side : 3 * side + 1, :] = total(jnp.where(at, down, 0))
+        slots[3 * side + 1 : 3 * side + 2, :] = total(jnp.where(at, turned[1 - side], 0))
+        slots[3 * side + 2 : 3 * side + 3, :] = jnp.maximum(below - 1, 0)
+        scales[2 * side : 2 * side + 1, :] = jnp.where((ordered == before) & ~first, 1.0, 0.0)
+        scales[2 * side + 1 : 2 * side + 2, :] = jnp.where(member > 0, 1.0, 0.0)
 
 
 def shards(n_row, n_col, block_values, block_index, block_count, strength, raw_scores):
     cap, size = block_values.shape[2], block_values.shape[3]
     seg, rhs, _ = raw_scores.shape
-    rows, cols = block_index[0, 0, 0], block_index[0, 0, 1]
-    count = block_count[0, 0]
     n_local, n_other = n_col * seg, n_row * seg
-    order_r, partner_r, follows_r, last_r, has_r = plan(rows, cols, count, n_local)
-    order_c, partner_c, follows_c, last_c, has_c = plan(cols, rows, count, n_other)
-    order = jnp.concatenate([order_r, partner_r, order_c, partner_c, last_r, last_c])
-    keep = jnp.concatenate([follows_r, follows_c, has_r, has_c]).astype(F32)
-    live = (jnp.arange(cap, dtype=jnp.int32) < count).astype(F32)[None, :]
-    gain = jnp.broadcast_to(strength[:, None], (rhs, size))
     field = (seg, rhs, size)
     vmem = pl.BlockSpec(memory_space=pltpu.VMEM)
     smem = pl.BlockSpec(memory_space=pltpu.SMEM)
@@ -431,20 +442,27 @@
     ]
     most = max(n_row, n_col)
     scratch += [
+        pltpu.VMEM((rhs, size), F32),
+        pltpu.VMEM((8, size), jnp.int32),
+        pltpu.VMEM((8, size), jnp.int32),
+        pltpu.VMEM((8, size), F32),
+        pltpu.SMEM((8, size), jnp.int32),
+        pltpu.SMEM((8, size), F32),
         pltpu.SemaphoreType.DMA,
+        pltpu.SemaphoreType.DMA((2,)),
         pltpu.SemaphoreType.DMA((7 * ITERS + 2, most)),
         pltpu.SemaphoreType.DMA((7 * ITERS + 2, most)),
     ]
     return pl.pallas_call(
         functools.partial(body, n_row, n_col),
         out_shape=(jax.ShapeDtypeStruct(field, F32), jax.ShapeDtypeStruct(field, F32)),
-        in_specs=[pl.BlockSpec(memory_space=pl.ANY), smem, smem, vmem, vmem, vmem, vmem],
+        in_specs=[pl.BlockSpec(memory_space=pl.ANY), vmem, vmem, smem, vmem],
         out_specs=(vmem, vmem),
         scratch_shapes=scratch,
         compiler_params=pltpu.CompilerParams(
             collective_id=0, has_side_effects=True, vmem_limit_bytes=56 * 1024 * 1024
         ),
-    )(block_values, order, keep, block_index[0, 0], live, gain, raw_scores)
+    )(block_values, block_index, block_count, strength, raw_scores)
 
 
 def solution(mesh):

time: 96.7 us -> 90.7 us (0.938)
  local copies, waits for them, and re-layouts: 5.59 us -> 2.75 us
  other arithmetic: 2.82 us -> 0 us
    broadcast_in_dim x1 -> x0, local copies, waits for them, and re-layouts: 1.33 us -> none  [shards(): gain = jnp.broadcast_to(strength[:, None], (rhs, size))]
    convert_element_type x2 -> x0, other arithmetic: 1.07 us -> none  [the longest x1 0.55 us: shards(): keep = jnp.concatenate([follows_r, follows_c, has_r, has_c]).astype(F32)]
where the time goes in v3:
time: 90.7 us; the launch traced here: 90.3 us
  Pallas kernels  86.3 us (95%)
  local copies, waits for them, and re-layouts  2.75 us (3%)
  between operations  1.28 us (1%)
    pallas_call x1, Pallas kernels, shards(): pl.pallas_call(functools.partial(body, n_row, n_col), out_shape=(jax.Shap...  86.3 us
    unnamed x2, local copies, waits for them, and re-layouts  2.75 us

profile of v3, /device:TPU:1, one launch (start us, length us, event | category | flops | bytes accessed | tf_op | source)
XLA Modules:
  0.0 90.3 jit_solution(9983709052050218002)
XLA Ops:
  1.3 86.3 %shard_map.68 = (f32[2,32,128]{2,1,0:T(8,128)}, f32[2,32,128]{2,1,0:T(8,128)}) custom-call(f32[1,1,40,128,128]{4,3,2,1,0:T(8,128)} %values_hbm.1, s32[1,1,2,40]{3,2,1,0:T(2,128)} %index_ref.1, s32[1,1]{1,0:T(1,128)S(6)} %copy.9.count_ref, f32[32]{0:T(128)} %strength_ref.1, f32[2,32,128]{2,1,0:T(8,128)} %raw_ref.1), custom_call_target="tpu_custom_call" | custom-call | tf_op jit(solution)/shard_map/pallas_call | solution.py:456
  87.6 1.4 %copy.10 = f32[2,32,128]{2,1,0:T(8,128)} copy(f32[2,32,128]{2,1,0:T(8,128)} %get-tuple-element.4) | data formatting | bytes 65536
  89.0 1.4 %copy.11 = f32[2,32,128]{2,1,0:T(8,128)} copy(f32[2,32,128]{2,1,0:T(8,128)} %get-tuple-element.5) | data formatting | bytes 65536

commit v4 on v3

--- a/solution.py
+++ b/solution.py
@@ -37,11 +37,11 @@
     count_ref,
     strength_ref,
     raw_ref,
-    smooth_ref,
-    resid_ref,
+    packed_ref,
     *scratch,
 ):
     names = iter(scratch)
+    smooth_ref, resid_ref = packed_ref.at[0], packed_ref.at[1]
     take = lambda: next(names)
     each_step = lambda: [take() for _ in range(ITERS)]
     stored, natural, turned, sums_row, sums_col = take(), take(), take(), take(), take()
@@ -117,7 +117,7 @@
         sums_col[pl.ds(q, 1), :] = jnp.sum(block, axis=0, keepdims=True)
         return 0
 
-    lax.fori_loop(0, cap // 2, prepare, 0, unroll=2)
+    lax.fori_loop(0, cap // 2, prepare, 0, unroll=10)
     pl.semaphore_wait(barrier, n_col + n_row - 2)
 
     def send(src, dst, target, which, out_slot, in_slot):
@@ -189,7 +189,7 @@
 
     gather(0)
 
-    lax.fori_loop(cap // 2, cap, prepare, 0, unroll=2)
+    lax.fori_loop(cap // 2, cap, prepare, 0, unroll=10)
 
     live = lax.broadcasted_iota(jnp.int32, (1, cap), 1) < count_ref[...]
 
@@ -225,7 +225,7 @@
             running[k] = total
             return total
 
-        lax.fori_loop(0, cap, slot, jnp.zeros((rhs, size), F32), unroll=4)
+        lax.fori_loop(0, cap, slot, jnp.zeros((rhs, size), F32), unroll=True)
 
     def total_of(ref, count):
         out = ref[0]
@@ -242,6 +242,7 @@
         kind = KINDS * step
         if step > 0:
             sends_done(step - 1)
+        pass_on(step)
         rows_above(lambda r: arrive(panel_cols[step].at[pl.ds(seg * r, seg)], kind + GATHER_ROW, r))
         pass_over(turned, panel_cols[step], 0)
         for k in far + [0]:
@@ -261,22 +262,6 @@
                 0,
                 z,
             )
-        for k in far + [0]:
-            z = lax.rem(chip + k, n_chip)
-            piece = pl.ds(seg * z, seg)
-            arrive(swap_got[step].at[piece], kind + SWAP, z)
-            for j in range(seg):
-                row_sum[step][seg * z + j] = row_send[step][core, seg * z + j] + swap_got[step][seg * z + j]
-            if k:
-                send(
-                    row_sum[step].at[piece],
-                    row_got[step].at[pl.ds(seg * chip, seg)],
-                    (a, 2 * z + core),
-                    kind + PART_COL,
-                    0,
-                    chip,
-                )
-        pass_on(step)
         from_sibling(step)
         if step == 0:
             arrive(deg_row_got.at[pl.ds(0, n_col - 1)], DEG_COL, 0)
@@ -305,6 +290,21 @@
         each_row(lambda r: send(dot_own[step], dot_row_got[step].at[a], (r, c), kind + DOT_ROW, 0, 0))
         dot_row_got[step][a] = dot_own[step][...]
 
+        for k in far + [0]:
+            z = lax.rem(chip + k, n_chip)
+            piece = pl.ds(seg * z, seg)
+            arrive(swap_got[step].at[piece], kind + SWAP, z)
+            for j in range(seg):
+                row_sum[step][seg * z + j] = row_send[step][core, seg * z + j] + swap_got[step][seg * z + j]
+            if k:
+                send(
+                    row_sum[step].at[piece],
+                    row_got[step].at[pl.ds(seg * chip, seg)],
+                    (a, 2 * z + core),
+                    kind + PART_COL,
+                    0,
+                    chip,
+                )
         pass_over(natural, panel_rows[step], 1)
         for v in range(n_other):
             col_send[step][v] = running[slots_at[5, v]] * scales_at[3, v]
@@ -453,16 +453,17 @@
         pltpu.SemaphoreType.DMA((7 * ITERS + 2, most)),
         pltpu.SemaphoreType.DMA((7 * ITERS + 2, most)),
     ]
-    return pl.pallas_call(
+    packed = pl.pallas_call(
         functools.partial(body, n_row, n_col),
-        out_shape=(jax.ShapeDtypeStruct(field, F32), jax.ShapeDtypeStruct(field, F32)),
+        out_shape=jax.ShapeDtypeStruct((2,) + field, F32),
         in_specs=[pl.BlockSpec(memory_space=pl.ANY), vmem, vmem, smem, vmem],
-        out_specs=(vmem, vmem),
+        out_specs=vmem,
         scratch_shapes=scratch,
         compiler_params=pltpu.CompilerParams(
             collective_id=0, has_side_effects=True, vmem_limit_bytes=56 * 1024 * 1024
         ),
     )(block_values, block_index, block_count, strength, raw_scores)
+    return packed[0], packed[1]
 
 
 def solution(mesh):

time: 90.7 us -> 81.7 us (0.901)
  Pallas kernels: 86.3 us -> 78.8 us
  local copies, waits for them, and re-layouts: 2.75 us -> 1.41 us
    pallas_call x1, Pallas kernels: 86.3 us -> 78.8 us  [shards(): pl.pallas_call(functools.partial(body, n_row, n_col), out_shape=jax.Shape...]
    unnamed x2 -> x0, local copies, waits for them, and re-layouts: 2.75 us -> none
    squeeze x0 -> x1, local copies, waits for them, and re-layouts: none -> 1.41 us  [shards(): return (packed[0], packed[1])]
where the time goes in v4:
time: 81.7 us; the launch traced here: 81.5 us
  Pallas kernels  78.8 us (96%)
  local copies, waits for them, and re-layouts  1.41 us (2%)
  between operations  1.28 us (2%)
    pallas_call x1, Pallas kernels, shards(): pl.pallas_call(functools.partial(body, n_row, n_col), out_shape=jax.Shape...  78.8 us

profile of v4, /device:TPU:1, one launch (start us, length us, event | category | flops | bytes accessed | tf_op | source)
XLA Modules:
  0.0 81.5 jit_solution(5342923143798399866)
XLA Ops:
  1.3 78.8 %shard_map.68 = f32[2,2,32,128]{3,2,1,0:T(8,128)} custom-call(f32[1,1,40,128,128]{4,3,2,1,0:T(8,128)} %values_hbm.1, s32[1,1,2,40]{3,2,1,0:T(2,128)} %index_ref.1, s32[1,1]{1,0:T(1,128)S(6)} %copy.7.count_ref, f32[32]{0:T(128)} %strength_ref.1, f32[2,32,128]{2,1,0:T(8,128)} %raw_ref.1), custom_call_target="tpu_custom_call" | custom-call | tf_op jit(solution)/shard_map/pallas_call | solution.py:456
  80.1 1.4 %slice_bitcast_fusion = (f32[2,32,128]{2,1,0:T(8,128)}, f32[2,32,128]{2,1,0:T(8,128)}) fusion(f32[2,2,32,128]{3,2,1,0:T(8,128)} %shard_map.68), kind=kLoop, calls=%fused_computation | loop fusion | bytes 131072 | tf_op jit(solution)/shard_map/squeeze | solution.py:466

commit v5 on v4

v5 whole, which is shorter than its diff:
```python
import functools

import jax
import jax.numpy as jnp
from jax import lax
from jax.experimental import pallas as pl
from jax.experimental.pallas import tpu as pltpu
from jax.sharding import PartitionSpec as P

ITERS = 3
PARTS = 2
MESH = pl.DeviceIdType.MESH
F32 = jnp.float32
BF16 = jnp.bfloat16


def split(x):
    high = x.astype(BF16)
    low = (x - high.astype(F32)).astype(BF16)
    return high, low


def product(field, weights):
    size = field.shape[0]
    width = field.shape[1]
    high, low = split(field)
    both = jnp.concatenate([high, low], axis=0)
    out = jnp.dot(both, weights, preferred_element_type=F32)
    upper = out[:size, :width]
    return upper + ((out[size:, :width] + out[:size, width:]) + out[size:, width:])


def body(
    n_row,
    n_col,
    values_hbm,
    index_ref,
    count_ref,
    strength_ref,
    raw_ref,
    packed_ref,
    *scratch,
):
    names = iter(scratch)
    take = lambda: next(names)
    each_step = lambda: [[take() for _ in range(PARTS)] for _ in range(ITERS)]
    stored, natural, turned, sums_row, sums_col = take(), take(), take(), take(), take()
    degree, direct, smooth = take(), take(), take()
    running = [take() for _ in range(PARTS)]
    got_rows, got_cols = each_step(), each_step()
    res_rows, res_cols = each_step(), each_step()
    row_send, col_send = each_step(), each_step()
    swap_got, row_sum = each_step(), each_step()
    row_got, col_got = each_step(), each_step()
    image = each_step()
    dot_own, dot_line = [take() for _ in range(ITERS)], [take() for _ in range(ITERS)]
    dot_col_got, dot_row_got = [take() for _ in range(ITERS)], [take() for _ in range(ITERS)]
    deg_row_send, deg_col_send, deg_row_got, deg_col_got = take(), take(), take(), take()
    gain_ref, listed, slots, scales, slots_at, scales_at = [take() for _ in range(6)]
    value_sem, plan_sem, sent, got = take(), take(), take(), take()

    a = lax.axis_index("row")
    c = lax.axis_index("col")
    core = lax.rem(c, 2)
    chip = c // 2
    sibling = c + 1 - 2 * core
    n_chip = n_col // 2
    far = sorted(range(1, n_chip), key=lambda k: -min(k, n_chip - k))
    cap = stored.shape[0]
    size = stored.shape[1]
    seg = raw_ref.shape[0]
    rhs = raw_ref.shape[1]
    share = rhs // PARTS
    n_local = n_col * seg
    n_other = n_row * seg
    GATHER_COL, GATHER_ROW, SWAP, PART_COL, PART_ROW = range(5)
    KINDS = 5
    DOTS = KINDS * PARTS * ITERS
    DEG_COL, DEG_ROW = DOTS + 2 * ITERS, DOTS + 2 * ITERS + 1
    sem_row = lambda step, part, kind: (step * PARTS + part) * KINDS + kind
    parts = range(PARTS)
    lanes = lambda part: slice(share * part, share * part + share)

    fetch = pltpu.make_async_copy(values_hbm.at[0, 0], stored, value_sem)
    fetch.start()

    barrier = pltpu.get_barrier_semaphore()

    def greet_col(k, _):
        pl.semaphore_signal(
            barrier, inc=1, device_id=(a, lax.rem(c + k, n_col)), device_id_type=MESH
        )
        return 0

    def greet_row(k, _):
        pl.semaphore_signal(
            barrier, inc=1, device_id=(lax.rem(a + k, n_row), c), device_id_type=MESH
        )
        return 0

    lax.fori_loop(1, n_col, greet_col, 0)
    lax.fori_loop(1, n_row, greet_row, 0)

    def send(src, dst, target, which, out_slot, in_slot):
        pltpu.make_async_remote_copy(
            src_ref=src,
            dst_ref=dst,
            send_sem=sent.at[which, out_slot],
            recv_sem=got.at[which, in_slot],
            device_id=target,
            device_id_type=MESH,
        ).start()

    def each_col(act):
        lax.fori_loop(1, n_col, lambda k, _: (act(lax.rem(c + k, n_col)), 0)[1], 0)

    def each_row(act):
        lax.fori_loop(1, n_row, lambda k, _: (act(lax.rem(a + k, n_row)), 0)[1], 0)

    def rows_below(act):
        lax.fori_loop(0, a, lambda k, _: (act(k), 0)[1], 0)

    def rows_above(act):
        lax.fori_loop(a + 1, n_row, lambda k, _: (act(k), 0)[1], 0)

    def other_chips(act):
        for k in far:
            act(lax.rem(chip + k, n_chip))

    def arrive(dst, which, slot):
        pltpu.make_async_copy(dst, dst, got.at[which, slot]).wait()

    def leave(src, which, slot):
        pltpu.make_async_copy(src, src, sent.at[which, slot]).wait()

    def gather(step, part):
        src = image[step][part]
        kind = sem_row(step, part, GATHER_COL)
        where = got_rows[step][part].at[pl.ds(seg * c, seg)]
        other_chips(lambda z: send(src, where, (a, 2 * z + core), kind, 0, c))
        send(src, where, (a, sibling), kind, 0, c)
        kind = sem_row(step, part, GATHER_ROW)
        where_col = got_cols[step][part].at[pl.ds(seg * a, seg)]
        rows_below(lambda r: send(src, where_col, (r, c), kind, r, a))
        got_rows[step][part][pl.ds(seg * c, seg)] = src[...]
        got_cols[step][part][pl.ds(seg * a, seg)] = src[...]

    def pass_on(step, part):
        kind = sem_row(step, part, GATHER_COL)
        for k in reversed(far):
            z = lax.rem(chip + k, n_chip)
            piece = got_rows[step][part].at[pl.ds(seg * (2 * z + core), seg)]
            arrive(piece, kind, 2 * z + core)
            send(piece, piece, (a, sibling), kind, 1, 2 * z + core)

    def from_sibling(step, part):
        kind = sem_row(step, part, GATHER_COL)
        for k in [0] + far[::-1]:
            z = lax.rem(chip + k, n_chip)
            slot = 2 * z + 1 - core
            arrive(got_rows[step][part].at[pl.ds(seg * slot, seg)], kind, slot)

    def sends_done(step):
        some = lambda ref, count: ref.at[pl.ds(0, count)]
        for part in parts:
            kind = sem_row(step, part, 0)
            leave(some(got_rows[step][part], seg * n_chip), kind + GATHER_COL, 0)
            leave(some(got_rows[step][part], seg * (n_chip - 1)), kind + GATHER_COL, 1)
            rows_below(lambda r: leave(image[step][part], kind + GATHER_ROW, r))
            leave(row_send[step][part].at[0], kind + SWAP, 0)
            leave(some(row_sum[step][part], seg * (n_chip - 1)), kind + PART_COL, 0)
            rows_above(lambda r: leave(some(col_send[step][part], seg), kind + PART_ROW, r))
        leave(some(dot_row_got[step], n_row - 1), DOTS + 2 * step, 0)
        leave(some(dot_col_got[step], n_col - 1), DOTS + 2 * step + 1, 0)

    for part in parts:
        image[0][part][...] = raw_ref[:, lanes(part), :]
    make_plan(index_ref, count_ref[...], cap, n_local, n_other, listed, slots, scales)
    to_slots = pltpu.make_async_copy(slots, slots_at, plan_sem.at[0])
    to_scales = pltpu.make_async_copy(scales, scales_at, plan_sem.at[1])
    to_slots.start()
    to_scales.start()
    for s in range(rhs):
        gain_ref[s : s + 1, :] = jnp.full((1, size), strength_ref[s], F32)
    fetch.wait()

    def prepare(q, _):
        block = stored[q]
        flipped = block.T
        high, low = split(block)
        natural[q, :, :size] = high
        natural[q, :, size:] = low
        high, low = split(flipped)
        turned[q, :, :size] = high
        turned[q, :, size:] = low
        sums_row[pl.ds(q, 1), :] = jnp.sum(flipped, axis=0, keepdims=True)
        sums_col[pl.ds(q, 1), :] = jnp.sum(block, axis=0, keepdims=True)
        return 0

    lax.fori_loop(0, cap // 2, prepare, 0, unroll=10)
    pl.semaphore_wait(barrier, n_col + n_row - 2)
    for part in parts:
        gather(0, part)
    lax.fori_loop(cap // 2, cap, prepare, 0, unroll=10)

    live = lax.broadcasted_iota(jnp.int32, (1, cap), 1) < count_ref[...]

    def pick(line, count):
        wanted = lax.broadcasted_iota(jnp.int32, (count, cap), 0)
        chosen = (wanted == index_ref[0, 0, line : line + 1, :]) & live
        return jnp.where(chosen, 1.0, 0.0)

    degree_rows = jnp.dot(
        pick(0, n_local), sums_row[...], precision=lax.Precision.HIGHEST, preferred_element_type=F32
    )
    degree_cols = jnp.dot(
        pick(1, n_other), sums_col[...], precision=lax.Precision.HIGHEST, preferred_element_type=F32
    )
    for peer in range(n_col):
        deg_row_send[peer] = degree_rows[seg * peer : seg * peer + seg, :]
    for peer in range(n_row):
        deg_col_send[peer] = degree_cols[seg * peer : seg * peer + seg, :]
    each_col(lambda p: send(deg_row_send.at[p], deg_row_got.at[c], (a, p), DEG_COL, 0, 0))
    rows_above(lambda r: send(deg_col_send.at[r], deg_col_got.at[a], (r, c), DEG_ROW, r, a))
    deg_row_got[c] = deg_row_send[c]
    deg_col_got[a] = deg_col_send[a]

    gains = gain_ref[...]
    to_slots.wait()
    to_scales.wait()

    def pass_over(weights, panel, side, out):
        def slot(k, total):
            weight = weights[slots_at[3 * side, k]]
            field = panel[slots_at[3 * side + 1, k]]
            total = total * scales_at[2 * side, k] + product(field, weight)
            out[k] = total
            return total

        lax.fori_loop(0, cap, slot, jnp.zeros((share, size), F32), unroll=True)

    def total_of(ref, count):
        out = ref[0]
        for k in range(1, count):
            out = out + ref[k]
        return out

    alphas, betas, gammas = [], [], []

    def finish_dots(step):
        arrive(dot_col_got[step].at[pl.ds(0, n_col - 1)], DOTS + 2 * step + 1, 0)
        dots = total_of(dot_col_got[step], n_col)
        dots = jnp.broadcast_to(dots, (size, size)).T
        gamma = dots[:rhs]
        delta = dots[rhs : 2 * rhs]
        if step == 0:
            alpha, beta = gamma / delta, None
        else:
            beta = gamma / gammas[-1]
            alpha = gamma / (delta - beta * gamma / alphas[-1])
        alphas.append(alpha)
        betas.append(beta)
        gammas.append(gamma)

    def form(step, part, fetched, formed, count):
        if step == 0:
            return fetched[0][part]
        alpha = alphas[step - 1][lanes(part)]
        before = fetched[0][part] if step == 1 else formed[step - 1][part]
        after = formed[step][part]

        if step == 1:
            def one(k, _):
                after[k] = before[k] - alpha * fetched[1][part][k]
                return 0
        else:
            beta = betas[step - 1][lanes(part)]

            def one(k, _):
                after[k] = before[k] - alpha * (fetched[2][part][k] + beta * fetched[1][part][k])
                return 0

        lax.fori_loop(0, count, one, 0, unroll=8)
        return after

    for step in range(ITERS):
        if step > 0:
            sends_done(step - 1)
            finish_dots(step - 1)
        gamma_part, delta_part, row_panels = [], [], []
        for part in parts:
            kind = sem_row(step, part, 0)
            pass_on(step, part)
            rows_above(lambda r: arrive(got_cols[step][part].at[pl.ds(seg * r, seg)], kind + GATHER_ROW, r))
            panel_cols = form(step, part, got_cols, res_cols, n_other)
            pass_over(turned, panel_cols, 0, running[part])
            for k in far + [0]:
                z = lax.rem(chip + k, n_chip)
                for half in range(2):
                    for j in range(seg):
                        u = seg * (2 * z + half) + j
                        row_send[step][part][half, seg * z + j] = (
                            running[part][slots_at[2, u]] * scales_at[1, u]
                        )
                piece = pl.ds(seg * z, seg)
                send(
                    row_send[step][part].at[1 - core, piece],
                    swap_got[step][part].at[piece],
                    (a, sibling),
                    kind + SWAP,
                    0,
                    z,
                )
            from_sibling(step, part)
            panel_rows = form(step, part, got_rows, res_rows, n_local)
            row_panels.append(panel_rows)
            pass_over(natural, panel_rows, 1, running[part])
            for v in range(n_other):
                col_send[step][part][v] = running[part][slots_at[5, v]] * scales_at[3, v]
            rows_above(
                lambda r: send(
                    col_send[step][part].at[pl.ds(seg * r, seg)],
                    col_got[step][part].at[pl.ds(seg * a, seg)],
                    (r, c),
                    kind + PART_ROW,
                    r,
                    a,
                )
            )
            col_got[step][part][pl.ds(seg * a, seg)] = col_send[step][part][pl.ds(seg * a, seg)]
            if part == PARTS - 1:
                if step == 0:
                    arrive(deg_row_got.at[pl.ds(0, n_col - 1)], DEG_COL, 0)
                    rows_below(lambda r: arrive(deg_col_got.at[r], DEG_ROW, r))
                    here = total_of(deg_row_got, n_col)
                    here = here + lax.fori_loop(
                        0, a + 1, lambda k, t: t + deg_col_got[k], jnp.zeros_like(here)
                    )
                    for j in range(seg):
                        degree[j] = jnp.broadcast_to(here[j : j + 1, :], (share, size))
                for p in parts:
                    cross = None
                    for u in range(n_local):
                        half, first = u // seg % 2, u // seg // 2 * seg
                        term = row_panels[p][u] * row_send[step][p][half, first + u % seg]
                        cross = term if cross is None else cross + term
                    square = [jnp.square(row_panels[p][seg * c + j]) for j in range(seg)]
                    gamma_part.append(functools.reduce(jnp.add, square))
                    rest = functools.reduce(jnp.add, [degree[j] * square[j] for j in range(seg)])
                    delta_part.append(gamma_part[p] + gains[lanes(p)] * (rest - 2.0 * cross))
                stack = jnp.concatenate(
                    gamma_part + delta_part + [jnp.zeros((size - 2 * rhs, size), F32)], axis=0
                )
                dot_own[step][...] = jnp.sum(stack.T, axis=0, keepdims=True)
                each_row(lambda r: send(dot_own[step], dot_row_got[step].at[a], (r, c), DOTS + 2 * step, 0, 0))
                dot_row_got[step][a] = dot_own[step][...]
            for k in far + [0]:
                z = lax.rem(chip + k, n_chip)
                piece = pl.ds(seg * z, seg)
                arrive(swap_got[step][part].at[piece], kind + SWAP, z)
                for j in range(seg):
                    row_sum[step][part][seg * z + j] = (
                        row_send[step][part][core, seg * z + j] + swap_got[step][part][seg * z + j]
                    )
                if k:
                    send(
                        row_sum[step][part].at[piece],
                        row_got[step][part].at[pl.ds(seg * chip, seg)],
                        (a, 2 * z + core),
                        kind + PART_COL,
                        0,
                        chip,
                    )

        fresh = []
        for part in parts:
            kind = sem_row(step, part, 0)
            if part == PARTS - 1:
                arrive(dot_row_got[step].at[pl.ds(0, n_row - 1)], DOTS + 2 * step, 0)
                dot_line[step][...] = total_of(dot_row_got[step], n_row)
                each_col(
                    lambda p: send(
                        dot_line[step], dot_col_got[step].at[c], (a, p), DOTS + 2 * step + 1, 0, 0
                    )
                )
                dot_col_got[step][c] = dot_line[step][...]
            rows_below(lambda r: arrive(col_got[step][part].at[pl.ds(seg * r, seg)], kind + PART_ROW, r))

            def add_cols(k, both):
                return tuple(both[j] + col_got[step][part][seg * k + j] for j in range(seg))

            spread = lax.fori_loop(
                0, a + 1, add_cols, tuple(row_sum[step][part][seg * chip + j] for j in range(seg))
            )
            spread = list(spread)
            for k in far[::-1]:
                z = lax.rem(chip + k, n_chip)
                arrive(row_got[step][part].at[pl.ds(seg * z, seg)], kind + PART_COL, z)
                for j in range(seg):
                    spread[j] = spread[j] + row_got[step][part][seg * z + j]
            w = []
            for j in range(seg):
                r = row_panels[part][seg * c + j]
                w.append(r + gains[lanes(part)] * (degree[j] * r - spread[j]))
            if step < ITERS - 1:
                for j in range(seg):
                    image[step + 1][part][j] = w[j]
                gather(step + 1, part)
            else:
                fresh.append(w)
        if step > 0:
            alpha, beta = alphas[step - 1], betas[step - 1]
            for part in parts:
                for j in range(seg):
                    own = (got_rows[0] if step == 1 else res_rows[step - 1])[part][seg * c + j]
                    if step == 1:
                        direct[j, lanes(part), :] = own
                        smooth[j, lanes(part), :] = alpha[lanes(part)] * own
                    else:
                        d = own + beta[lanes(part)] * direct[j, lanes(part), :]
                        direct[j, lanes(part), :] = d
                        smooth[j, lanes(part), :] = smooth[j, lanes(part), :] + alpha[lanes(part)] * d

    finish_dots(ITERS - 1)
    for part in parts:
        alpha, beta = alphas[-1][lanes(part)], betas[-1][lanes(part)]
        for j in range(seg):
            r = row_panels[part][seg * c + j]
            slope = image[2][part][j] + betas[1][lanes(part)] * image[1][part][j]
            slope = fresh[part][j] + beta * slope
            d = r + beta * direct[j, lanes(part), :]
            packed_ref[0, j, lanes(part), :] = smooth[j, lanes(part), :] + alpha * d
            packed_ref[1, j, lanes(part), :] = r - alpha * slope
    sends_done(ITERS - 1)
    leave(deg_row_got.at[pl.ds(0, n_col - 1)], DEG_COL, 0)
    rows_above(lambda r: leave(deg_col_send.at[r], DEG_ROW, r))


def make_plan(index_ref, count, cap, n_local, n_other, listed, slots, scales):
    width = listed.shape[1]
    listed[...] = jnp.zeros_like(listed)
    listed[0:2, 0:cap] = index_ref[0, 0]
    down = lax.broadcasted_iota(jnp.int32, (width, width), 0)
    across = lax.broadcasted_iota(jnp.int32, (width, width), 1)
    lines = [jnp.broadcast_to(listed[j : j + 1, :], (width, width)) for j in range(2)]
    turned = [line.T for line in lines]
    for side, groups in enumerate((n_local, n_other)):
        key = jnp.where(across < count, lines[side], groups) * width + across
        group = jnp.where(down < count, turned[side], groups)
        key_down = group * width + down
        rank = jnp.sum(jnp.where(key < key_down, 1, 0), axis=1, keepdims=True)
        at = rank == across
        total = lambda x: jnp.sum(x, axis=0, keepdims=True)
        ordered = total(jnp.where(at, group, 0))
        before = pltpu.roll(ordered, 1, 1)
        first = across[0:1, :] == 0
        below = total(jnp.where(group <= across, 1, 0))
        member = total(jnp.where(group == across, 1, 0))
        slots[3 * side : 3 * side + 1, :] = total(jnp.where(at, down, 0))
        slots[3 * side + 1 : 3 * side + 2, :] = total(jnp.where(at, turned[1 - side], 0))
        slots[3 * side + 2 : 3 * side + 3, :] = jnp.maximum(below - 1, 0)
        scales[2 * side : 2 * side + 1, :] = jnp.where((ordered == before) & ~first, 1.0, 0.0)
        scales[2 * side + 1 : 2 * side + 2, :] = jnp.where(member > 0, 1.0, 0.0)


def shards(n_row, n_col, block_values, block_index, block_count, strength, raw_scores):
    cap, size = block_values.shape[2], block_values.shape[3]
    seg, rhs, _ = raw_scores.shape
    n_local, n_other = n_col * seg, n_row * seg
    field = (seg, rhs, size)
    vmem = pl.BlockSpec(memory_space=pltpu.VMEM)
    smem = pl.BlockSpec(memory_space=pltpu.SMEM)
    n_chip = n_col // 2
    share = rhs // PARTS
    whole = lambda shape: [pltpu.VMEM(shape, F32)]
    many = lambda count: [pltpu.VMEM((count, share, size), F32) for _ in range(ITERS * PARTS)]
    scratch = [
        pltpu.VMEM((cap, size, size), F32),
        pltpu.VMEM((cap, size, 2 * size), BF16),
        pltpu.VMEM((cap, size, 2 * size), BF16),
        pltpu.VMEM((cap, size), F32),
        pltpu.VMEM((cap, size), F32),
        pltpu.VMEM((seg, share, size), F32),
        pltpu.VMEM(field, F32),
        pltpu.VMEM(field, F32),
    ]
    scratch += whole((cap, share, size)) * PARTS
    scratch += many(n_local) + many(n_other)
    scratch += many(n_local) + many(n_other)
    scratch += whole((2, n_chip * seg, share, size)) * (ITERS * PARTS) + many(n_other)
    scratch += many(n_chip * seg) + many(n_chip * seg)
    scratch += many(n_chip * seg) + many(n_other)
    scratch += many(seg)
    scratch += whole((1, size)) * (2 * ITERS)
    scratch += whole((n_col, 1, size)) * ITERS + whole((n_row, 1, size)) * ITERS
    scratch += [
        pltpu.VMEM((n_col, seg, size), F32),
        pltpu.VMEM((n_row, seg, size), F32),
        pltpu.VMEM((n_col, seg, size), F32),
        pltpu.VMEM((n_row, seg, size), F32),
    ]
    most = max(n_row, n_col)
    rows = 5 * PARTS * ITERS + 2 * ITERS + 2
    scratch += [
        pltpu.VMEM((rhs, size), F32),
        pltpu.VMEM((8, size), jnp.int32),
        pltpu.VMEM((8, size), jnp.int32),
        pltpu.VMEM((8, size), F32),
        pltpu.SMEM((8, size), jnp.int32),
        pltpu.SMEM((8, size), F32),
        pltpu.SemaphoreType.DMA,
        pltpu.SemaphoreType.DMA((2,)),
        pltpu.SemaphoreType.DMA((rows, most)),
        pltpu.SemaphoreType.DMA((rows, most)),
    ]
    packed = pl.pallas_call(
        functools.partial(body, n_row, n_col),
        out_shape=jax.ShapeDtypeStruct((2,) + field, F32),
        in_specs=[pl.BlockSpec(memory_space=pl.ANY), vmem, vmem, smem, vmem],
        out_specs=vmem,
        scratch_shapes=scratch,
        compiler_params=pltpu.CompilerParams(
            collective_id=0, has_side_effects=True, vmem_limit_bytes=56 * 1024 * 1024
        ),
    )(block_values, block_index, block_count, strength, raw_scores)
    return packed[0], packed[1]


def solution(mesh):
    n_row, n_col = mesh.shape["row"], mesh.shape["col"]
    placed = (
        P("row", "col", None, None, None),
        P("row", "col", None, None),
        P("row", "col"),
        P(),
        P(("row", "col"), None, None),
    )
    return jax.shard_map(
        functools.partial(shards, n_row, n_col),
        mesh=mesh,
        in_specs=placed,
        out_specs=(P(("row", "col"), None, None), P(("row", "col"), None, None)),
        check_vma=False,
    )
```

time: 81.7 us -> 78.5 us (0.961)
  Pallas kernels: 78.8 us -> 75.5 us
    pallas_call x1, Pallas kernels: 78.8 us -> 75.5 us  [shards(): pl.pallas_call(functools.partial(body, n_row, n_col), out_shape=jax.Shape...]
where the time goes in v5:
time: 78.5 us; the launch traced here: 78.2 us
  Pallas kernels  75.5 us (96%)
  local copies, waits for them, and re-layouts  1.41 us (2%)
  between operations  1.28 us (2%)
    pallas_call x1, Pallas kernels, shards(): pl.pallas_call(functools.partial(body, n_row, n_col), out_shape=jax.Shape...  75.5 us

profile of v5, /device:TPU:1, one launch (start us, length us, event | category | flops | bytes accessed | tf_op | source)
XLA Modules:
  0.0 78.2 jit_solution(9950643196470629322)
XLA Ops:
  1.3 75.5 %shard_map.68 = f32[2,2,32,128]{3,2,1,0:T(8,128)} custom-call(f32[1,1,40,128,128]{4,3,2,1,0:T(8,128)} %values_hbm.1, s32[1,1,2,40]{3,2,1,0:T(2,128)} %index_ref.1, s32[1,1]{1,0:T(1,128)S(6)} %copy.7.count_ref, f32[32]{0:T(128)} %strength_ref.1, f32[2,32,128]{2,1,0:T(8,128)} %raw_ref.1), custom_call_target="tpu_custom_call" | custom-call | tf_op jit(solution)/shard_map/pallas_call | solution.py:516
  76.8 1.4 %slice_bitcast_fusion = (f32[2,32,128]{2,1,0:T(8,128)}, f32[2,32,128]{2,1,0:T(8,128)}) fusion(f32[2,2,32,128]{3,2,1,0:T(8,128)} %shard_map.68), kind=kLoop, calls=%fused_computation | loop fusion | bytes 131072 | tf_op jit(solution)/shard_map/squeeze | solution.py:526

commit v6 on v5

--- a/solution.py
+++ b/solution.py
@@ -170,8 +170,8 @@
             leave(row_send[step][part].at[0], kind + SWAP, 0)
             leave(some(row_sum[step][part], seg * (n_chip - 1)), kind + PART_COL, 0)
             rows_above(lambda r: leave(some(col_send[step][part], seg), kind + PART_ROW, r))
-        leave(some(dot_row_got[step], n_row - 1), DOTS + 2 * step, 0)
-        leave(some(dot_col_got[step], n_col - 1), DOTS + 2 * step + 1, 0)
+        leave(some(dot_col_got[step], n_col - 1), DOTS + 2 * step, 0)
+        leave(some(dot_row_got[step], n_row - 1), DOTS + 2 * step + 1, 0)
 
     for part in parts:
         image[0][part][...] = raw_ref[:, lanes(part), :]
@@ -248,8 +248,8 @@
     alphas, betas, gammas = [], [], []
 
     def finish_dots(step):
-        arrive(dot_col_got[step].at[pl.ds(0, n_col - 1)], DOTS + 2 * step + 1, 0)
-        dots = total_of(dot_col_got[step], n_col)
+        arrive(dot_row_got[step].at[pl.ds(0, n_row - 1)], DOTS + 2 * step + 1, 0)
+        dots = total_of(dot_row_got[step], n_row)
         dots = jnp.broadcast_to(dots, (size, size)).T
         gamma = dots[:rhs]
         delta = dots[rhs : 2 * rhs]
@@ -352,8 +352,8 @@
                     gamma_part + delta_part + [jnp.zeros((size - 2 * rhs, size), F32)], axis=0
                 )
                 dot_own[step][...] = jnp.sum(stack.T, axis=0, keepdims=True)
-                each_row(lambda r: send(dot_own[step], dot_row_got[step].at[a], (r, c), DOTS + 2 * step, 0, 0))
-                dot_row_got[step][a] = dot_own[step][...]
+                each_col(lambda p: send(dot_own[step], dot_col_got[step].at[c], (a, p), DOTS + 2 * step, 0, 0))
+                dot_col_got[step][c] = dot_own[step][...]
             for k in far + [0]:
                 z = lax.rem(chip + k, n_chip)
                 piece = pl.ds(seg * z, seg)
@@ -376,14 +376,14 @@
         for part in parts:
             kind = sem_row(step, part, 0)
             if part == PARTS - 1:
-                arrive(dot_row_got[step].at[pl.ds(0, n_row - 1)], DOTS + 2 * step, 0)
-                dot_line[step][...] = total_of(dot_row_got[step], n_row)
-                each_col(
-                    lambda p: send(
-                        dot_line[step], dot_col_got[step].at[c], (a, p), DOTS + 2 * step + 1, 0, 0
+                arrive(dot_col_got[step].at[pl.ds(0, n_col - 1)], DOTS + 2 * step, 0)
+                dot_line[step][...] = total_of(dot_col_got[step], n_col)
+                each_row(
+                    lambda r: send(
+                        dot_line[step], dot_row_got[step].at[a], (r, c), DOTS + 2 * step + 1, 0, 0
                     )
                 )
-                dot_col_got[step][c] = dot_line[step][...]
+                dot_row_got[step][a] = dot_line[step][...]
             rows_below(lambda r: arrive(col_got[step][part].at[pl.ds(seg * r, seg)], kind + PART_ROW, r))
 
             def add_cols(k, both):
@@ -421,6 +421,9 @@
                         direct[j, lanes(part), :] = d
                         smooth[j, lanes(part), :] = smooth[j, lanes(part), :] + alpha[lanes(part)] * d
 
+    sends_done(ITERS - 1)
+    leave(deg_row_got.at[pl.ds(0, n_col - 1)], DEG_COL, 0)
+    rows_above(lambda r: leave(deg_col_send.at[r], DEG_ROW, r))
     finish_dots(ITERS - 1)
     for part in parts:
         alpha, beta = alphas[-1][lanes(part)], betas[-1][lanes(part)]
@@ -431,9 +434,6 @@
             d = r + beta * direct[j, lanes(part), :]
             packed_ref[0, j, lanes(part), :] = smooth[j, lanes(part), :] + alpha * d
             packed_ref[1, j, lanes(part), :] = r - alpha * slope
-    sends_done(ITERS - 1)
-    leave(deg_row_got.at[pl.ds(0, n_col - 1)], DEG_COL, 0)
-    rows_above(lambda r: leave(deg_col_send.at[r], DEG_ROW, r))
 
 
 def make_plan(index_ref, count, cap, n_local, n_other, listed, slots, scales):

time: 78.5 us -> 77.4 us (0.986)
  Pallas kernels: 75.5 us -> 74.4 us
    pallas_call x1, Pallas kernels: 75.5 us -> 74.4 us  [shards(): pl.pallas_call(functools.partial(body, n_row, n_col), out_shape=jax.Shape...]
where the time goes in v6:
time: 77.4 us; the launch traced here: 77.1 us
  Pallas kernels  74.4 us (96%)
  local copies, waits for them, and re-layouts  1.41 us (2%)
  between operations  1.28 us (2%)
    pallas_call x1, Pallas kernels, shards(): pl.pallas_call(functools.partial(body, n_row, n_col), out_shape=jax.Shape...  74.4 us

profile of v6, /device:TPU:1, one launch (start us, length us, event | category | flops | bytes accessed | tf_op | source)
XLA Modules:
  0.0 77.1 jit_solution(11685011441180039449)
XLA Ops:
  1.3 74.4 %shard_map.68 = f32[2,2,32,128]{3,2,1,0:T(8,128)} custom-call(f32[1,1,40,128,128]{4,3,2,1,0:T(8,128)} %values_hbm.1, s32[1,1,2,40]{3,2,1,0:T(2,128)} %index_ref.1, s32[1,1]{1,0:T(1,128)S(6)} %copy.7.count_ref, f32[32]{0:T(128)} %strength_ref.1, f32[2,32,128]{2,1,0:T(8,128)} %raw_ref.1), custom_call_target="tpu_custom_call" | custom-call | tf_op jit(solution)/shard_map/pallas_call | solution.py:516
  75.7 1.4 %slice_bitcast_fusion = (f32[2,32,128]{2,1,0:T(8,128)}, f32[2,32,128]{2,1,0:T(8,128)}) fusion(f32[2,2,32,128]{3,2,1,0:T(8,128)} %shard_map.68), kind=kLoop, calls=%fused_computation | loop fusion | bytes 131072 | tf_op jit(solution)/shard_map/squeeze | solution.py:526

commit v7 on v6

--- a/solution.py
+++ b/solution.py
@@ -314,6 +314,32 @@
             from_sibling(step, part)
             panel_rows = form(step, part, got_rows, res_rows, n_local)
             row_panels.append(panel_rows)
+            if part == PARTS - 1 and step == ITERS - 1:
+                if step == 0:
+                    arrive(deg_row_got.at[pl.ds(0, n_col - 1)], DEG_COL, 0)
+                    rows_below(lambda r: arrive(deg_col_got.at[r], DEG_ROW, r))
+                    here = total_of(deg_row_got, n_col)
+                    here = here + lax.fori_loop(
+                        0, a + 1, lambda k, t: t + deg_col_got[k], jnp.zeros_like(here)
+                    )
+                    for j in range(seg):
+                        degree[j] = jnp.broadcast_to(here[j : j + 1, :], (share, size))
+                for p in parts:
+                    cross = None
+                    for u in range(n_local):
+                        half, first = u // seg % 2, u // seg // 2 * seg
+                        term = row_panels[p][u] * row_send[step][p][half, first + u % seg]
+                        cross = term if cross is None else cross + term
+                    square = [jnp.square(row_panels[p][seg * c + j]) for j in range(seg)]
+                    gamma_part.append(functools.reduce(jnp.add, square))
+                    rest = functools.reduce(jnp.add, [degree[j] * square[j] for j in range(seg)])
+                    delta_part.append(gamma_part[p] + gains[lanes(p)] * (rest - 2.0 * cross))
+                stack = jnp.concatenate(
+                    gamma_part + delta_part + [jnp.zeros((size - 2 * rhs, size), F32)], axis=0
+                )
+                dot_own[step][...] = jnp.sum(stack.T, axis=0, keepdims=True)
+                each_col(lambda p: send(dot_own[step], dot_col_got[step].at[c], (a, p), DOTS + 2 * step, 0, 0))
+                dot_col_got[step][c] = dot_own[step][...]
             pass_over(natural, panel_rows, 1, running[part])
             for v in range(n_other):
                 col_send[step][part][v] = running[part][slots_at[5, v]] * scales_at[3, v]
@@ -328,7 +354,7 @@
                 )
             )
             col_got[step][part][pl.ds(seg * a, seg)] = col_send[step][part][pl.ds(seg * a, seg)]
-            if part == PARTS - 1:
+            if part == PARTS - 1 and step < ITERS - 1:
                 if step == 0:
                     arrive(deg_row_got.at[pl.ds(0, n_col - 1)], DEG_COL, 0)
                     rows_below(lambda r: arrive(deg_col_got.at[r], DEG_ROW, r))

time: 77.4 us -> 77.6 us (level)
  no operation moved by 1% of the time
where the time goes in v7:
time: 77.6 us; the launch traced here: 77.4 us
  Pallas kernels  74.7 us (96%)
  local copies, waits for them, and re-layouts  1.41 us (2%)
  between operations  1.28 us (2%)
    pallas_call x1, Pallas kernels, shards(): pl.pallas_call(functools.partial(body, n_row, n_col), out_shape=jax.Shape...  74.7 us

profile of v7, /device:TPU:1, one launch (start us, length us, event | category | flops | bytes accessed | tf_op | source)
XLA Modules:
  0.0 77.4 jit_solution(4004890082529485887)
XLA Ops:
  1.3 74.7 %shard_map.68 = f32[2,2,32,128]{3,2,1,0:T(8,128)} custom-call(f32[1,1,40,128,128]{4,3,2,1,0:T(8,128)} %values_hbm.1, s32[1,1,2,40]{3,2,1,0:T(2,128)} %index_ref.1, s32[1,1]{1,0:T(1,128)S(6)} %copy.7.count_ref, f32[32]{0:T(128)} %strength_ref.1, f32[2,32,128]{2,1,0:T(8,128)} %raw_ref.1), custom_call_target="tpu_custom_call" | custom-call | tf_op jit(solution)/shard_map/pallas_call | solution.py:542
  76.0 1.4 %slice_bitcast_fusion = (f32[2,32,128]{2,1,0:T(8,128)}, f32[2,32,128]{2,1,0:T(8,128)}) fusion(f32[2,2,32,128]{3,2,1,0:T(8,128)} %shard_map.68), kind=kLoop, calls=%fused_computation | loop fusion | bytes 131072 | tf_op jit(solution)/shard_map/squeeze | solution.py:552
